TPU v7x, 128 devices: a whole 4x4x4 slice. The times are simulated.
128 devices in a mesh: seg: 8 (over x, core), sec: 16 (over z, y).
Axes of the slice: x: 4, y: 4, z: 4, core: 2. Of those that a mesh axis runs over, the one named last changes fastest.
Arguments:
- left_environment: bfloat16 [8, 128, 64, 1920], P('seg', 'sec'), may hold values from -0.125 to 0.125
- right_environment: bfloat16 [8, 128, 64, 1920], P('seg', 'sec'), may hold values from -0.75 to 0.75
- site_previous: bfloat16 [8, 128, 64, 256], P('seg', 'sec'), may hold values from -0.75 to 0.75
- state_start: float32 [8, 128, 64, 256], P('seg', 'sec'), may hold values from -36 to 36
- preconditioner: float32 [8, 128, 64, 256], P('seg', 'sec'), may hold values from 0.25 to 4
- channel_tensor: bfloat16 [30, 4, 30, 4], replicated, may hold values from -0.5 to 0.5
- channel_mask: int32 [30, 30], replicated, may hold values 0 or 1
- sector_shift: int32 [5, 128], replicated, may hold values from 0 to 127, as said below
- left_sizes: int32 [128], replicated, may hold values from 32 to 64, as said below
- right_sizes: int32 [128, 4], replicated, may hold values from 32 to 64, as said below
Outputs:
- bond_state: float32 [8, 128, 64, 256], P('seg', 'sec')
- energy: float32 [8], P('seg')
Inputs may be any that keep to these rules, and one draw needn't show every extreme that they name: Each row is a permutation of the 128 sectors; for every group of 8 consecutive sectors and every other such group, at most 3 pairs of a class k and a sector l of the first group have sector_shift[k, l] in the second group, and some pair of groups reaches 3. `left_sizes`: some sector fills its tile and some has 32 live states. `right_sizes`: some block fills its tile and some has 32 live states.
All inputs are finite; a program needn't handle non-finite values.
Results may differ from a plain program's by a relative error of at most 0.012.
Values may be sent and summed in bfloat16 or wider, within the bound.
No kernel may reach another device: no remote copies, remote signals or barrier semaphores. Data moves between devices by JAX's collectives and lax.ppermute only.
A program may use at most 256 MiB of HBM per device.

v0:
```python
import jax
import jax.numpy as jnp
from jax import lax
from jax.sharding import PartitionSpec as P

W = 30
D = 4
B = 64
SEC_DEV = 8
CLASSES = 5
ITERS = 2


EPSILON = 1e-06
HIGHEST_PRECISION = lax.Precision.HIGHEST


def passed_along(block, axis, distance):
    devices = range(lax.axis_size(axis))
    route = [(i - distance, i) for i in devices if i - distance in devices]
    return lax.ppermute(block, axis, route)


def live_masks(left_sizes, right_sizes, offset):
    row_limit = lax.dynamic_slice_in_dim(left_sizes, offset, SEC_DEV, 0)
    column_limit = lax.dynamic_slice_in_dim(right_sizes, offset, SEC_DEV, 0)
    row_live = jnp.arange(B, dtype=jnp.int32)[None, :] < row_limit[:, None]
    column_live = jnp.arange(B, dtype=jnp.int32)[None, None, :] < column_limit[:, :, None]
    joined_live = row_live[:, :, None, None] & column_live[:, None, :, :]
    return joined_live.astype(jnp.float32).reshape(SEC_DEV, B, D * B)


def pair_layout(sector_shift, group):
    target_list = lax.dynamic_slice_in_dim(sector_shift, group * SEC_DEV, SEC_DEV, 1).T.reshape(
        SEC_DEV * CLASSES
    )
    owner_list = target_list // SEC_DEV
    order = jnp.arange(SEC_DEV * CLASSES, dtype=jnp.int32)
    earlier = order[None, :] < order[:, None]
    same_target = target_list[:, None] == target_list[None, :]
    leading = jnp.logical_not(jnp.any(same_target & earlier, axis=1))
    rank_list = jnp.sum(
        ((owner_list[:, None] == owner_list[None, :]) & earlier).astype(jnp.int32), axis=1
    )
    return (target_list, owner_list, leading, rank_list, same_target)


def build_environment(environment, site_blocks, channel_mix, sector_shift, offset):
    every_site = lax.all_gather(site_blocks, "sec", axis=0, tiled=True)
    groups = W // CLASSES
    split_left = environment.reshape(SEC_DEV, B, CLASSES, groups, B)
    own_tensor = site_blocks.reshape(SEC_DEV, B, D, B)
    every_tensor = every_site.reshape(every_site.shape[0], B, D, B)
    contracted = jnp.einsum(
        "lpkja,lasb->lpkjsb", split_left, own_tensor, preferred_element_type=jnp.float32
    ).astype(jnp.bfloat16)
    channel_split = channel_mix.reshape(CLASSES, groups, D, W, D)
    accumulated = jnp.zeros((SEC_DEV, B, W, B), jnp.float32)
    for charge in range(CLASSES):
        targets = lax.dynamic_slice_in_dim(sector_shift[charge], offset, SEC_DEV, 0)
        shifted_site = jnp.take(every_tensor, targets, axis=0)
        carried = jnp.einsum(
            "jtvs,lpjsb->lptvb",
            channel_split[charge],
            contracted[:, :, charge],
            preferred_element_type=jnp.float32,
        ).astype(jnp.bfloat16)
        accumulated = accumulated + jnp.einsum(
            "lpte,lptvb->levb", shifted_site, carried, preferred_element_type=jnp.float32
        )
    return accumulated.astype(jnp.bfloat16).reshape(SEC_DEV, B, W * B)


def apply_operator(vector_low, left_split, right_split, channel_mix, routing, live_mask):
    blocks = vector_low.reshape(SEC_DEV, B, D, B)
    right_product = jnp.einsum(
        "lasb,lbvc->lasvc", blocks, right_split, preferred_element_type=jnp.float32
    ).astype(jnp.bfloat16)
    mixed_product = jnp.einsum(
        "wtvs,lasvc->lwatc", channel_mix, right_product, preferred_element_type=jnp.float32
    ).astype(jnp.bfloat16)
    grouped = mixed_product.reshape(SEC_DEV, CLASSES, W // CLASSES, B, D, B)
    partial_value = jnp.einsum(
        "lpkja,lkjatc->lkptc", left_split, grouped, preferred_element_type=jnp.float32
    )
    partial_value = partial_value.reshape(SEC_DEV * CLASSES, B * D * B)
    onehot, send_matrix, take_matrix = routing
    every_row = jnp.dot(
        onehot, partial_value, precision=HIGHEST_PRECISION, preferred_element_type=jnp.float32
    )
    reduced = lax.psum(every_row.astype(jnp.bfloat16), "sec").astype(jnp.float32)
    summed = lax.dynamic_slice_in_dim(reduced, lax.axis_index("sec") * SEC_DEV, SEC_DEV, 0)
    return live_mask * summed.reshape(SEC_DEV, B, D * B)


def on_device(
    left_environment,
    right_environment,
    site_previous,
    state_start,
    preconditioner,
    channel_tensor,
    channel_mask,
    sector_shift,
    left_sizes,
    right_sizes,
):
    group_total = lax.axis_size("sec")
    my_group = lax.axis_index("sec")
    offset = my_group * SEC_DEV
    sectors = SEC_DEV * group_total
    capacity = (CLASSES * SEC_DEV + group_total - 1) // group_total
    channel_mix = channel_tensor * channel_mask.astype(jnp.bfloat16)[:, None, :, None]
    live_mask = live_masks(left_sizes, right_sizes, offset)
    own_left = left_environment[0]
    fresh = build_environment(own_left, site_previous[0], channel_mix, sector_shift, offset)
    handed = passed_along(fresh, "seg", 1)
    position = lax.axis_index("seg")
    left_used = jnp.where(position == 0, own_left, handed)
    came_right = passed_along(right_environment[0], "seg", -1)
    right_used = jnp.where(position == lax.axis_size("seg") - 1, right_environment[0], came_right)
    left_split = left_used.reshape(SEC_DEV, B, CLASSES, W // CLASSES, B)
    right_split = right_used.reshape(SEC_DEV, B, W, B)
    target_list, owner_list, leading, rank_list, same_target = pair_layout(sector_shift, my_group)
    onehot = (jnp.arange(sectors, dtype=jnp.int32)[:, None] == target_list[None, :]).astype(
        jnp.float32
    )
    merge_matrix = (leading[:, None] & same_target).astype(jnp.float32)
    slot_owner = jnp.repeat(jnp.arange(group_total, dtype=jnp.int32), capacity)
    slot_rank = jnp.tile(jnp.arange(capacity, dtype=jnp.int32), group_total)
    slot_matrix = (
        (owner_list[None, :] == slot_owner[:, None]) & (rank_list[None, :] == slot_rank[:, None])
    ).astype(jnp.float32)
    send_matrix = jnp.dot(
        slot_matrix, merge_matrix, precision=HIGHEST_PRECISION, preferred_element_type=jnp.float32
    )
    every_target, every_owner, every_leading, every_rank, unused_same = jax.vmap(
        lambda group: pair_layout(sector_shift, group)
    )(jnp.arange(group_total, dtype=jnp.int32))
    local_target = every_target - offset
    hits = (every_owner == my_group) & every_leading
    take_table = (
        hits[:, None, None, :]
        & (
            every_rank[:, None, None, :]
            == jnp.arange(capacity, dtype=jnp.int32)[None, None, :, None]
        )
        & (
            local_target[:, None, None, :]
            == jnp.arange(SEC_DEV, dtype=jnp.int32)[None, :, None, None]
        )
    )
    take_matrix = jnp.sum(take_table.astype(jnp.float32), axis=3)
    take_matrix = (
        jnp.transpose(take_matrix, (1, 0, 2))
        .reshape(SEC_DEV, group_total * capacity)
        .astype(jnp.bfloat16)
    )
    routing = (onehot, send_matrix, take_matrix)
    total_entries = float(SEC_DEV * B * D * B * group_total)

    def operator(vector):
        return apply_operator(
            vector.astype(jnp.bfloat16), left_split, right_split, channel_mix, routing, live_mask
        )

    def rayleigh(vector, result):
        return lax.psum(jnp.sum(vector * result), "sec") / total_entries

    current = live_mask * state_start[0]
    start_square = lax.psum(jnp.sum(current * current), "sec") / total_entries
    current = current / jnp.sqrt(start_square + EPSILON)
    applied = operator(current)
    precondition = preconditioner[0]
    for iteration in range(ITERS):
        rayleigh_value = rayleigh(current, applied)
        correction = precondition * (applied - rayleigh_value * current)
        correlation_value = lax.psum(jnp.sum(current * correction), "sec") / total_entries
        correction = correction - correlation_value * current
        squared_length = lax.psum(jnp.sum(correction * correction), "sec") / total_entries
        direction = correction / jnp.sqrt(squared_length + EPSILON)
        product = operator(direction)
        sums = lax.psum(
            (
                jnp.sum(current * product),
                jnp.sum(direction * applied),
                jnp.sum(direction * product),
            ),
            "sec",
        )
        cross_term = 0.5 * (sums[0] + sums[1]) / total_entries
        far_term = sums[2] / total_entries
        rotation = 0.5 * jnp.arctan2(-2.0 * cross_term, far_term - rayleigh_value)
        cosine = jnp.cos(rotation)
        sine = jnp.sin(rotation)
        current = cosine * current + sine * direction
        applied = cosine * applied + sine * product
    energy_value = rayleigh(current, applied)
    return (current[None], jnp.reshape(energy_value, (1,)))


def solution(mesh):
    in_specs = (
        P("seg", "sec", None, None),
        P("seg", "sec", None, None),
        P("seg", "sec", None, None),
        P("seg", "sec", None, None),
        P("seg", "sec", None, None),
        P(),
        P(),
        P(),
        P(),
        P(),
    )
    out_specs = (P("seg", "sec", None, None), P("seg"))
    return jax.shard_map(
        on_device, mesh=mesh, in_specs=in_specs, out_specs=out_specs, check_vma=False
    )
```

profile of v0, /device:TPU:2, one launch (start us, length us, event | category | flops | bytes accessed | tf_op | source)
XLA Modules:
  0.0 1331.9 jit_solution(96695211588679389)
XLA Ops:
  22.6 43.7 %psum.119 = f32[]{:T(128)} all-reduce(f32[]{:T(128)} %multiply_reduce_fusion.13), channel_id=1, replica_groups=mesh['seg'=8,'sec'=16] {'sec'}, use_global_device_ids=true, to_apply=%region_1.2 | all-reduce | flops 1 | bytes 8 | tf_op jit(solution)/shard_map/psum | solution.py:171
  189.9 16.8 %fusion.20 = f32[8,64,30,64,1]{3,1,4,2,0:T(8,128)S(1)} fusion(bf16[8,64,4,30,64]{4,3,2,1,0:T(8,128)(2,1)} %fusion.4, bf16[8,64,4,64]{3,1,2,0:T(8,128)(2,1)S(1)} %gather_fusion.4, pred[8]{0:T(512)(128)(4,1)S(1)} %get-tuple-element.28), kind=kOutput, calls=%fused_computation.36 | convolution fusion | flops 503447552 | bytes 12058632 | tf_op jit(solution)/shard_map/lpte,lptvb->levb/dot_general | solution.py:68
  206.7 18.2 %fusion.22 = f32[8,64,30,64,1]{3,1,4,2,0:T(8,128)} fusion(bf16[8,64,4,30,64]{4,3,2,1,0:T(8,128)(2,1)} %fusion.3, bf16[8,64,4,64]{3,1,2,0:T(8,128)(2,1)S(1)} %gather_fusion.3, pred[8]{0:T(512)(128)(4,1)S(1)} %get-tuple-element.40), kind=kOutput, calls=%fused_computation.38 | convolution fusion | flops 503447552 | bytes 12058632 | tf_op jit(solution)/shard_map/lpte,lptvb->levb/dot_general | solution.py:68
  224.9 18.7 %fusion.24 = f32[8,64,30,64,1]{3,1,4,2,0:T(8,128)} fusion(bf16[8,64,4,30,64]{4,3,2,1,0:T(8,128)(2,1)} %fusion.2, bf16[8,64,4,64]{3,1,2,0:T(8,128)(2,1)S(1)} %gather_fusion.2, pred[8]{0:T(512)(128)(4,1)S(1)} %get-tuple-element.24), kind=kOutput, calls=%fused_computation.40 | convolution fusion | flops 503447552 | bytes 12058632 | tf_op jit(solution)/shard_map/lpte,lptvb->levb/dot_general | solution.py:68
  243.6 18.5 %fusion.26 = f32[8,64,30,64,1]{3,1,4,2,0:T(8,128)} fusion(bf16[8,64,4,30,64]{4,3,2,1,0:T(8,128)(2,1)} %fusion.1, bf16[8,64,4,64]{3,1,2,0:T(8,128)(2,1)S(1)} %gather_fusion.1, pred[8]{0:T(512)(128)(4,1)S(1)} %get-tuple-element.42), kind=kOutput, calls=%fused_computation.42 | convolution fusion | flops 503447552 | bytes 12058632 | tf_op jit(solution)/shard_map/lpte,lptvb->levb/dot_general | solution.py:68
  262.1 23.9 %fusion.36 = bf16[8,64,30,64]{3,1,2,0:T(8,128)(2,1)S(1)} fusion(f32[8,64,30,64,1]{3,1,4,2,0:T(8,128)S(1)} %fusion.20, f32[8,64,30,64,1]{3,1,4,2,0:T(8,128)} %fusion.22, f32[8,64,30,64,1]{3,1,4,2,0:T(8,128)} %fusion.24, f32[8,64,30,64,1]{3,1,4,2,0:T(8,128)} %fusion.26, bf16[8,64,4,30,64]{4,3,2,1,0:T(8,128)(2,1)} %fusion, ...), kind=kOutput, calls=%fused_computation.51 | convolution fusion | flops 508362752 | bytes 25821192 | tf_op jit(solution)/shard_map/lpte,lptvb->levb/dot_general | solution.py:68
  309.5 46.9 %fusion.5 = bf16[8,30,64,4,64]{4,1,3,2,0:T(8,128)(2,1)} fusion(bf16[8,64,4,30,64,1]{4,1,3,2,0,5:T(8,128)(2,1)} %convert_bitcast_fusion.2, bf16[30,4,30,4,1,1]{2,3,0,1,5,4:T(4,128)(2,1)S(1)} %fusion.135), kind=kOutput, calls=%fused_computation.21 | convolution fusion | flops 947650560 | bytes 15757440 | tf_op jit(solution)/shard_map/wtvs,lasvc->lwatc/dot_general | solution.py:79
  356.3 18.4 %copy.243 = bf16[8,30,64,4,64]{4,2,3,1,0:T(8,128)(2,1)} copy(bf16[8,30,64,4,64]{4,1,3,2,0:T(8,128)(2,1)} %fusion.5) | data formatting | bytes 15728640 | tf_op jit(solution)/shard_map/convert_element_type | solution.py:81
  420.1 101.2 %all-reduce.6.cloned.1.call-done = bf16[128,16384]{1,0:T(8,128)(2,1)} async-done(((bf16[128,16384]{1,0:T(8,128)(2,1)}), bf16[128,16384]{1,0:T(8,128)(2,1)}) %all-reduce.6.cloned.1.call-update) | async-done | bytes 4194320 | tf_op jit(solution)/shard_map/psum | solution.py:91
  524.7 39.0 %psum.121 = f32[]{:T(128)} all-reduce(f32[]{:T(128)} %multiply_reduce_fusion.12), channel_id=1, replica_groups=mesh['seg'=8,'sec'=16] {'sec'}, use_global_device_ids=true, to_apply=%region_4.6 | all-reduce | flops 1 | bytes 8 | tf_op jit(solution)/shard_map/psum | solution.py:168
  566.9 36.1 %psum.122 = f32[]{:T(128)} all-reduce(f32[]{:T(128)} %multiply_reduce_fusion.11), channel_id=1, replica_groups=mesh['seg'=8,'sec'=16] {'sec'}, use_global_device_ids=true, to_apply=%region_6.8 | all-reduce | flops 1 | bytes 8 | tf_op jit(solution)/shard_map/psum | solution.py:178
  605.4 38.1 %psum.123 = f32[]{:T(128)} all-reduce(f32[]{:T(128)} %get-tuple-element.18), channel_id=1, replica_groups=mesh['seg'=8,'sec'=16] {'sec'}, use_global_device_ids=true, to_apply=%region_8.10 | all-reduce | flops 1 | bytes 8 | tf_op jit(solution)/shard_map/psum | solution.py:180
  656.9 47.1 %fusion.6 = bf16[8,30,64,4,64]{4,1,3,2,0:T(8,128)(2,1)} fusion(bf16[8,64,4,30,64,1]{4,1,3,2,0,5:T(8,128)(2,1)} %convert_bitcast_fusion.1, bf16[30,4,30,4,1,1]{2,3,0,1,5,4:T(4,128)(2,1)S(1)} %fusion.135), kind=kOutput, calls=%fused_computation.22 | convolution fusion | flops 947650560 | bytes 15757440 | tf_op jit(solution)/shard_map/wtvs,lasvc->lwatc/dot_general | solution.py:79
  703.9 18.3 %copy.252 = bf16[8,30,64,4,64]{4,2,3,1,0:T(8,128)(2,1)} copy(bf16[8,30,64,4,64]{4,1,3,2,0:T(8,128)(2,1)} %fusion.6) | data formatting | bytes 15728640 | tf_op jit(solution)/shard_map/convert_element_type | solution.py:81
  757.2 100.2 %all-reduce.8.cloned.1.call-done = bf16[128,16384]{1,0:T(8,128)(2,1)} async-done(((bf16[128,16384]{1,0:T(8,128)(2,1)}), bf16[128,16384]{1,0:T(8,128)(2,1)}) %all-reduce.8.cloned.1.call-update) | async-done | bytes 4194320 | tf_op jit(solution)/shard_map/psum | solution.py:91
  862.0 39.3 %all-reduce.1 = (f32[]{:T(128)}, f32[]{:T(128)}) all-reduce(f32[]{:T(128)S(6)} %add.117, f32[]{:T(128)} %get-tuple-element.5), channel_id=1, replica_groups=mesh['seg'=8,'sec'=16] {'sec'}, use_global_device_ids=true, to_apply=%region_11.13 | all-reduce | flops 2 | bytes 16 | tf_op jit(solution)/shard_map/psum | solution.py:183
  906.0 36.1 %psum.128 = f32[]{:T(128)} all-reduce(f32[]{:T(128)} %get-tuple-element.15), channel_id=1, replica_groups=mesh['seg'=8,'sec'=16] {'sec'}, use_global_device_ids=true, to_apply=%region_17.19 | all-reduce | flops 1 | bytes 8 | tf_op jit(solution)/shard_map/psum | solution.py:168
  946.3 38.1 %psum.129 = f32[]{:T(128)} all-reduce(f32[]{:T(128)} %multiply_reduce_fusion.5), channel_id=1, replica_groups=mesh['seg'=8,'sec'=16] {'sec'}, use_global_device_ids=true, to_apply=%region_19.21 | all-reduce | flops 1 | bytes 8 | tf_op jit(solution)/shard_map/psum | solution.py:178
  987.8 36.1 %psum.130 = f32[]{:T(128)} all-reduce(f32[]{:T(128)} %get-tuple-element.13), channel_id=1, replica_groups=mesh['seg'=8,'sec'=16] {'sec'}, use_global_device_ids=true, to_apply=%region_21.23 | all-reduce | flops 1 | bytes 8 | tf_op jit(solution)/shard_map/psum | solution.py:180
  1036.0 46.9 %fusion.7 = bf16[8,30,64,4,64]{4,1,3,2,0:T(8,128)(2,1)} fusion(bf16[8,64,4,30,64,1]{4,1,3,2,0,5:T(8,128)(2,1)} %convert_bitcast_fusion, bf16[30,4,30,4,1,1]{2,3,0,1,5,4:T(4,128)(2,1)S(1)} %fusion.135), kind=kOutput, calls=%fused_computation.23 | convolution fusion | flops 947650560 | bytes 15757440 | tf_op jit(solution)/shard_map/wtvs,lasvc->lwatc/dot_general | solution.py:79
  1082.9 18.0 %copy.261 = bf16[8,30,64,4,64]{4,2,3,1,0:T(8,128)(2,1)} copy(bf16[8,30,64,4,64]{4,1,3,2,0:T(8,128)(2,1)} %fusion.7) | data formatting | bytes 15728640 | tf_op jit(solution)/shard_map/convert_element_type | solution.py:81
  1136.2 101.7 %all-reduce.10.cloned.1.call-done = bf16[128,16384]{1,0:T(8,128)(2,1)} async-done(((bf16[128,16384]{1,0:T(8,128)(2,1)}), bf16[128,16384]{1,0:T(8,128)(2,1)}) %all-reduce.10.cloned.1.call-update) | async-done | bytes 4194320 | tf_op jit(solution)/shard_map/psum | solution.py:91
  1243.1 39.0 %all-reduce = (f32[]{:T(128)}, f32[]{:T(128)}) all-reduce(f32[]{:T(128)S(6)} %add.123, f32[]{:T(128)} %get-tuple-element.3), channel_id=1, replica_groups=mesh['seg'=8,'sec'=16] {'sec'}, use_global_device_ids=true, to_apply=%region_24.26 | all-reduce | flops 2 | bytes 16 | tf_op jit(solution)/shard_map/psum | solution.py:183
  1287.3 36.1 %psum.135 = f32[]{:T(128)} all-reduce(f32[]{:T(128)} %multiply_reduce_fusion), channel_id=1, replica_groups=mesh['seg'=8,'sec'=16] {'sec'}, use_global_device_ids=true, to_apply=%region_30.32 | all-reduce | flops 1 | bytes 8 | tf_op jit(solution)/shard_map/psum | solution.py:168
  (125 shorter events, 329.4 us)
Async XLA Ops:
  7.2 13.7 %copy-start = (s32[128,4]{0,1:T(4,128)S(1)}, s32[128,4]{0,1:T(4,128)}, u32[]{:S(2)}) copy-start(s32[128,4]{0,1:T(4,128)} %param.21) | copy-start | bytes 6148
  7.2 13.5 %copy-start.15 = (s32[128]{0:T(128)S(1)}, s32[128]{0:T(128)}, u32[]{:S(2)}) copy-start(s32[128]{0:T(128)} %param.20) | copy-start | bytes 1540
  7.2 14.1 %copy-start.2 = (f32[1,8,64,256]{3,2,1,0:T(8,128)S(1)}, f32[1,8,64,256]{3,2,1,0:T(8,128)}, u32[]{:S(2)}) copy-start(f32[1,8,64,256]{3,2,1,0:T(8,128)} %param.15) | copy-start | bytes 1572868
  7.2 141.9 %all-gather.3.cloned.1.call-start = ((), (), s32[]{:S(2)}) async-start(), calls=%async_computation.3 | async-start | bytes 4456448 | tf_op jit(solution)/shard_map/all_gather | solution.py:49
  7.9 513.4 %all-reduce.6.cloned.1.call-start = ((), (), s32[]{:S(2)}) async-start(), calls=%async_computation | async-start | bytes 8388608 | tf_op jit(solution)/shard_map/psum | solution.py:91
  8.0 130.6 %collective-permute-start.1 = (bf16[8,64,1920]{2,1,0:T(8,128)(2,1)}, bf16[8,64,1920]{2,1,0:T(8,128)(2,1)}, u32[]{:S(2)}, u32[]{:S(2)}) collective-permute-start(bf16[8,64,1920]{2,1,0:T(8,128)(2,1)} %bitcast.339), channel_id=1, source_target_pairs={{16,0},{32,16},{48,32},{64,48},{80,64},{96,80},{112,96},{17,1},{33... | collective-permute-start | bytes 5898248 | tf_op jit(solution)/shard_map/ppermute | solution.py:21
  21.8 56.0 %copy-start.12 = (pred[8,256]{1,0:T(8,128)(4,1)}, pred[8,256]{1,0:T(8,128)(4,1)S(1)}, u32[]{:S(2)}) copy-start(pred[8,256]{1,0:T(8,128)(4,1)S(1)} %broadcast_compare_fusion) | copy-start | bytes 6148
  67.7 10.1 copy-start.11
  129.7 8.9 copy-start.10
  243.6 18.5 %copy-start.9 = (bf16[8,64,4,64]{3,1,2,0:T(8,128)(2,1)S(1)}, bf16[8,64,4,64]{3,1,2,0:T(8,128)(2,1)}, u32[]{:S(2)}) copy-start(bf16[8,64,4,64]{3,1,2,0:T(8,128)(2,1)} %gather_fusion) | copy-start | bytes 786436
  297.2 77.6 %collective-permute-start = (bf16[8,64,1920]{2,1,0:T(8,128)(2,1)}, bf16[8,64,1920]{2,1,0:T(8,128)(2,1)}, u32[]{:S(2)}, u32[]{:S(2)}) collective-permute-start(bf16[8,64,1920]{2,1,0:T(8,128)(2,1)} %reshape.160), channel_id=1, source_target_pairs={{0,16},{16,32},{32,48},{48,64},{64,80},{80,96},{96,112},{1,17},{17... | collective-permute-start | bytes 5898248 | tf_op jit(solution)/shard_map/ppermute | solution.py:21
  356.3 18.4 %copy-start.7 = (bf16[1,8,64,1920]{3,2,1,0:T(8,128)(2,1)S(1)}, bf16[1,8,64,1920]{3,2,1,0:T(8,128)(2,1)}, u32[]{:S(2)}) copy-start(bf16[1,8,64,1920]{3,2,1,0:T(8,128)(2,1)} %param.12) | copy-start | bytes 5898244
  406.7 6.2 copy-start.14
  412.9 109.4 %copy-start.3 = (f32[1,8,64,256]{3,2,1,0:T(8,128)S(1)}, f32[1,8,64,256]{3,2,1,0:T(8,128)}, u32[]{:S(2)}) copy-start(f32[1,8,64,256]{3,2,1,0:T(8,128)} %param.15) | copy-start | bytes 1572868
  412.9 109.4 %copy-start.13 = (pred[8,256]{1,0:T(8,128)(4,1)S(1)}, pred[8,256]{1,0:T(8,128)(4,1)}, u32[]{:S(2)}) copy-start(pred[8,256]{1,0:T(8,128)(4,1)} %copy-done.12) | copy-start | bytes 6148
  412.9 110.3 %copy-start.4 = (f32[1,8,64,256]{3,2,1,0:T(8,128)S(1)}, f32[1,8,64,256]{3,2,1,0:T(8,128)}, u32[]{:S(2)}) copy-start(f32[1,8,64,256]{3,2,1,0:T(8,128)} %param.16) | copy-start | bytes 1572868
  420.0 437.4 %all-reduce.8.cloned.1.call-start = ((), (), s32[]{:S(2)}) async-start(), calls=%async_computation.1 | async-start | bytes 8388608 | tf_op jit(solution)/shard_map/psum | solution.py:91
  757.2 480.6 %all-reduce.10.cloned.1.call-start = ((), (), s32[]{:S(2)}) async-start(), calls=%async_computation.2 | async-start | bytes 8388608 | tf_op jit(solution)/shard_map/psum | solution.py:91
  1129.1 110.6 %copy-start.5 = (f32[8,64,256]{2,1,0:T(8,128)S(1)}, f32[8,64,256]{2,1,0:T(8,128)}, u32[]{:S(2)}) copy-start(f32[8,64,256]{2,1,0:T(8,128)} %get-tuple-element.16) | copy-start | bytes 1572868
  1129.1 110.6 %copy-start.6 = (f32[8,64,256]{2,1,0:T(8,128)S(1)}, f32[8,64,256]{2,1,0:T(8,128)}, u32[]{:S(2)}) copy-start(f32[8,64,256]{2,1,0:T(8,128)} %get-tuple-element.17) | copy-start | bytes 1572868
  1136.1 187.9 %copy-start.1 = (s32[128,4]{0,1:T(4,128)S(1)}, s32[128,4]{0,1:T(4,128)}, u32[]{:S(2)}) copy-start(s32[128,4]{0,1:T(4,128)} %param.21) | copy-start | bytes 6148
  1238.8 0.8 copy-start.8
Sparse Core Ops, SparseCore 0:
  10.2 54.2 all-gather.2
  420.2 101.1 all-reduce.5
  757.3 100.0 all-reduce.7
  1136.3 101.5 all-reduce.9
where the time goes:
time: 1340 us; the launch traced here: 1330 us
  matrix products  388 us (29%)
  blocking collectives  381 us (28%)
  waiting for transfers between devices  304 us (23%)
  local copies, waits for them, and re-layouts  197 us (15%)
  other arithmetic  30.9 us (2%)
  between operations  26.5 us (2%)
    psum x3, waiting for transfers between devices, apply_operator(): lax.psum(every_row.astype(jnp.bfloat16), 'sec').astype(jnp.float32)  303 us
    dot_general x3, matrix products, apply_operator(): jnp.einsum('wtvs,lasvc->lwatc', channel_mix, right_product, preferred_ele...  141 us
    psum x3, blocking collectives, rayleigh(): return lax.psum(jnp.sum(vector * result), 'sec') / total_entries  111 us
    dot_general x5, matrix products, build_environment(): jnp.einsum('lpte,lptvb->levb', shifted_site, carried, preferred_element_t...  96 us
    psum x2, blocking collectives, on_device(): lax.psum((jnp.sum(current * product), jnp.sum(direction * applied), jnp.s...  78.3 us
    psum x2, blocking collectives, on_device(): lax.psum(jnp.sum(current * correction), 'sec') / total_entries  74.2 us
    psum x2, blocking collectives, on_device(): lax.psum(jnp.sum(correction * correction), 'sec') / total_entries  74.1 us
    convert_element_type x3, local copies, waits for them, and re-layouts, apply_operator(): mixed_product = jnp.einsum('wtvs,lasvc->lwatc', channel_mix, right_produc...  54.7 us
  transfers between devices with their start and end apart: 6, of which 3 were waited for; matrix products, arithmetic and copies ran while one was open for 13% of the time, Pallas kernels for 0%

commit v1 on v0

v1 whole, which is shorter than its diff:
```python
import functools

import jax
import jax.numpy as jnp
from jax import lax
from jax.experimental import pallas as pl
from jax.experimental.pallas import tpu as pltpu
from jax.sharding import PartitionSpec as P

W = 30
D = 4
B = 64
SEC_DEV = 8
CLASSES = 5
GROUP = W // CLASSES
PAIRS = SEC_DEV * CLASSES
HALF = B // 2
FOLD = 2 * B
ROWS = W * HALF
TILE = D * HALF
MIX = 128
EPSILON = 1e-06
BF = jnp.bfloat16
F32 = jnp.float32


def passed_along(block, axis, distance):
    devices = range(lax.axis_size(axis))
    route = [(i - distance, i) for i in devices if i - distance in devices]
    return lax.ppermute(block, axis, route)


def low_lanes(rows):
    return lax.broadcasted_iota(jnp.int32, (rows, FOLD), 1) < B


def fold_pair(pair):
    stacked = jnp.concatenate([pair, pltpu.roll(pair, FOLD - HALF, 1)], axis=0)
    turned = stacked.T
    return turned[:HALF], turned[B : B + HALF]


def unfold_pair(first, second):
    filler = jnp.zeros((HALF, FOLD), F32)
    turned = jnp.concatenate([first, filler, second, filler], axis=0).T
    upper = lax.broadcasted_iota(jnp.int32, (B, FOLD), 1) % B < HALF
    return jnp.where(upper, turned[:B], pltpu.roll(turned[B:], HALF, 1))


def spread(tile):
    rolled = pltpu.roll(tile, B, 1)
    low = low_lanes(HALF)
    zero = jnp.zeros_like(tile)
    return jnp.concatenate(
        [
            jnp.where(low, tile, zero),
            jnp.where(low, rolled, zero),
            jnp.where(low, zero, rolled),
            jnp.where(low, zero, tile),
        ],
        axis=0,
    )


def spread_pair(pair):
    rolled = pltpu.roll(pair, B, 1)
    low = low_lanes(B)
    zero = jnp.zeros_like(pair)
    first = jnp.concatenate([jnp.where(low, pair, zero), jnp.where(low, zero, rolled)], axis=0)
    second = jnp.concatenate([jnp.where(low, rolled, zero), jnp.where(low, zero, pair)], axis=0)
    return first, second


def dot(left, right):
    return jnp.dot(left, right, preferred_element_type=F32)


def route_kernel(me_ref, shift_ref, site_ref, slot_ref, local_ref, take_ref, send_ref, count, source):
    groups = send_ref.shape[0]
    slots = send_ref.shape[1]
    me = me_ref[0]
    for g in range(groups):
        count[g] = 0
    for i in range(groups * slots):
        source[i] = 0
    for l in range(SEC_DEV):
        for k in range(CLASSES):
            target = shift_ref[k, me * SEC_DEV + l]
            owner = target // SEC_DEV
            rank = count[owner]
            count[owner] = rank + 1
            slot = owner * slots + jnp.minimum(rank, slots - 1)
            slot_ref[l * CLASSES + k] = jnp.where(owner == me, -1, slot)
            local_ref[l * CLASSES + k] = target % SEC_DEV

    def one_group(g, carry):
        rank = jnp.int32(0)
        for l in range(SEC_DEV):
            for k in range(CLASSES):
                target = shift_ref[k, g * SEC_DEV + l]
                hit = target // SEC_DEV == me
                place = jnp.minimum(rank, slots - 1)

                @pl.when(hit)
                def _():
                    local = target % SEC_DEV
                    take_ref[k * SEC_DEV + local] = jnp.where(g == me, -1, g * slots + place)
                    source[g * slots + place] = local

                rank = rank + hit.astype(jnp.int32)
        return carry

    lax.fori_loop(0, groups, one_group, 0)

    def one_copy(g, carry):
        for r in range(slots):
            send_ref[g, r] = site_ref[source[g * slots + r]]
        return carry

    lax.fori_loop(0, groups, one_copy, 0)


def route(me, sector_shift, site, groups, slots):
    smem = pl.BlockSpec(memory_space=pltpu.SMEM)
    vmem = pl.BlockSpec(memory_space=pltpu.VMEM)
    return pl.pallas_call(
        route_kernel,
        out_shape=(
            jax.ShapeDtypeStruct((PAIRS,), jnp.int32),
            jax.ShapeDtypeStruct((PAIRS,), jnp.int32),
            jax.ShapeDtypeStruct((PAIRS,), jnp.int32),
            jax.ShapeDtypeStruct((groups, slots, B, D * B), BF),
        ),
        in_specs=[smem, smem, vmem],
        out_specs=(smem, smem, smem, vmem),
        scratch_shapes=[pltpu.SMEM((groups,), jnp.int32), pltpu.SMEM((groups * slots,), jnp.int32)],
        name="route",
    )(me, sector_shift, site)


def fold_environment_kernel(in_ref, out_ref):
    for i in range(W // 2):
        pair = in_ref[0, :, i * FOLD : (i + 1) * FOLD].astype(F32)
        first, second = fold_pair(pair)
        out_ref[0, (2 * i) * HALF : (2 * i + 1) * HALF, :] = first.astype(BF)
        out_ref[0, (2 * i + 1) * HALF : (2 * i + 2) * HALF, :] = second.astype(BF)


def fold_environment(environment):
    return pl.pallas_call(
        fold_environment_kernel,
        grid=(SEC_DEV,),
        out_shape=jax.ShapeDtypeStruct((SEC_DEV, ROWS, FOLD), BF),
        in_specs=[pl.BlockSpec((1, B, W * B), lambda l: (l, 0, 0))],
        out_specs=pl.BlockSpec((1, ROWS, FOLD), lambda l: (l, 0, 0)),
        name="fold_environment",
        cost_estimate=pl.CostEstimate(flops=0, bytes_accessed=4 * SEC_DEV * ROWS * FOLD, transcendentals=0),
    )(environment)


def live_mask(left_size, right_sizes):
    half_p = lax.broadcasted_iota(jnp.int32, (HALF, FOLD), 1)
    column = lax.broadcasted_iota(jnp.int32, (HALF, FOLD), 0) + jnp.where(half_p < B, 0, HALF)
    row = jnp.where(half_p < B, half_p, half_p - B)
    parts = [
        jnp.where((row < left_size) & (column < right_sizes[t]), 1.0, 0.0).astype(F32) for t in range(D)
    ]
    return jnp.concatenate(parts, axis=0)


def fold_state_kernel(left_ref, right_ref, state_ref, weight_ref, start_ref, fold_ref):
    l = pl.program_id(0)
    mask = live_mask(left_ref[l], [right_ref[l * D + t] for t in range(D)])
    for source, result in ((state_ref, start_ref), (weight_ref, fold_ref)):
        tiles = []
        for i in range(D // 2):
            tiles.extend(fold_pair(source[0, :, i * FOLD : (i + 1) * FOLD]))
        folded = jnp.concatenate(tiles, axis=0)
        result[0] = mask * folded if result is start_ref else folded


def fold_state(left_sizes, right_sizes, state, weight):
    natural = pl.BlockSpec((1, B, D * B), lambda l, *refs: (l, 0, 0))
    folded = pl.BlockSpec((1, TILE, FOLD), lambda l, *refs: (l, 0, 0))
    shape = jax.ShapeDtypeStruct((SEC_DEV, TILE, FOLD), F32)
    return pl.pallas_call(
        fold_state_kernel,
        out_shape=(shape, shape),
        grid_spec=pltpu.PrefetchScalarGridSpec(
            num_scalar_prefetch=2,
            grid=(SEC_DEV,),
            in_specs=[natural, natural],
            out_specs=(folded, folded),
        ),
        name="fold_state",
        cost_estimate=pl.CostEstimate(flops=0, bytes_accessed=16 * SEC_DEV * TILE * FOLD, transcendentals=0),
    )(left_sizes, right_sizes, state, weight)


def mix_channels(mix, first, second):
    for j in range(0, HALF, 2):
        parts = [first[pl.ds(j + i, MIX, stride=HALF), :].astype(BF) for i in range(2)]
        mixed = dot(mix, jnp.concatenate(parts, axis=1))
        for i in range(2):
            second[pl.ds(j + i, MIX, stride=HALF), :] = mixed[:, i * FOLD : (i + 1) * FOLD]


def build_kernel(slot_ref, local_ref, env_ref, own_ref, came_ref, mix_ref, out_ref, first, second):
    l = pl.program_id(0)

    @pl.when(l == 0)
    def _():
        first[W * D * HALF :, :] = jnp.zeros((MIX * HALF - W * D * HALF, FOLD), F32)

    mix_turned = mix_ref[...].astype(F32).T.astype(BF)
    for k in range(CLASSES):
        slot = slot_ref[l * CLASSES + k]
        local = local_ref[l * CLASSES + k]
        tensor = jnp.where(slot < 0, own_ref[local], came_ref[jnp.maximum(slot, 0)])
        blocks = []
        for i in range(D // 2):
            blocks.extend(spread_pair(tensor[:, i * FOLD : (i + 1) * FOLD].astype(F32)))
        right = jnp.concatenate(blocks, axis=1).astype(BF)
        left = env_ref[0, k * GROUP * HALF : (k + 1) * GROUP * HALF, :]
        joined = dot(left, right)
        for j in range(GROUP):
            for t in range(D):
                at = ((k * GROUP + j) * D + t) * HALF
                first[at : at + HALF, :] = joined[j * HALF : (j + 1) * HALF, t * FOLD : (t + 1) * FOLD]
    mix_channels(mix_turned, first, second)
    own = own_ref[l]
    tiles = []
    low_half = low_lanes(HALF)
    for i in range(D // 2):
        pair = own[:, i * FOLD : (i + 1) * FOLD].astype(F32)
        rolled = pltpu.roll(pair, B, 1)
        tiles.append(jnp.where(low_half, pair[:HALF], rolled[HALF:]))
        tiles.append(jnp.where(low_half, rolled[:HALF], pair[HALF:]))
    turned = jnp.concatenate(tiles, axis=0).T.astype(BF)
    low = low_lanes(B)
    for v in range(0, W, 2):
        right = jnp.concatenate(
            [second[(v + i) * TILE : (v + i + 1) * TILE, :].astype(BF) for i in range(2)], axis=1
        )
        product = dot(turned, right)
        for i in range(2):
            block = product[:, i * FOLD : (i + 1) * FOLD]
            chosen = jnp.where(low, block[:B], block[B:])
            total = chosen + pltpu.roll(chosen, B, 1)
            folded = jnp.where(low_half, total[:HALF], total[HALF:])
            out_ref[0, (v + i) * HALF : (v + i + 1) * HALF, :] = folded.astype(BF)


def build_environment(slot, local, environment, site, came, mix):
    folded = pl.BlockSpec((1, ROWS, FOLD), lambda l, *refs: (l, 0, 0))
    whole = lambda shape: pl.BlockSpec(shape, lambda l, *refs: (0,) * len(shape))
    return pl.pallas_call(
        build_kernel,
        out_shape=jax.ShapeDtypeStruct((SEC_DEV, ROWS, FOLD), BF),
        grid_spec=pltpu.PrefetchScalarGridSpec(
            num_scalar_prefetch=2,
            grid=(SEC_DEV,),
            in_specs=[folded, whole(site.shape), whole(came.shape), whole(mix.shape)],
            out_specs=folded,
            scratch_shapes=[pltpu.VMEM((MIX * HALF, FOLD), F32), pltpu.VMEM((MIX * HALF, FOLD), F32)],
        ),
        name="build_environment",
        cost_estimate=pl.CostEstimate(flops=10**10, bytes_accessed=10**7, transcendentals=0),
    )(slot, local, environment, site, came, mix)


def gram_sums(gram_ref, entries):
    total = gram_ref[0]
    for g in range(1, gram_ref.shape[0]):
        total = total + gram_ref[g]
    row = total[:1] * (1.0 / entries)
    lane = lax.broadcasted_iota(jnp.int32, (1, FOLD), 1)
    return lambda i: jnp.sum(jnp.where(lane == i, row, 0.0), axis=1, keepdims=True)


def rotation(cross_sum, far, rayleigh_value):
    up, along = -cross_sum, far - rayleigh_value
    scale = jnp.maximum(jnp.abs(up), jnp.abs(along))
    flat = scale == 0.0
    scale = jnp.where(flat, 1.0, scale)
    up, along = up / scale, along / scale
    length = jnp.sqrt(up * up + along * along)
    length = jnp.where(flat, 1.0, length)
    larger = jnp.sqrt(0.5 * (1.0 + jnp.abs(along) / length))
    smaller = jnp.abs(up) / (2.0 * length * larger)
    ahead = along >= 0.0
    cosine = jnp.where(flat, 1.0, jnp.where(ahead, larger, smaller))
    size = jnp.where(ahead, smaller, larger)
    sine = jnp.where(flat, 0.0, jnp.where(cross_sum < 0.0, size, -size))
    return cosine, sine


def correction_scalars(xx, xa, xpa, xpx, papa, papx, pxpx):
    along = xpa - xa * xpx
    square = papa - 2.0 * xa * papx + xa * xa * pxpx
    square = square - 2.0 * along * along + along * along * xx
    return xa, along, lax.rsqrt(jnp.maximum(square, 0.0) + EPSILON)


FIRST = ("uu", "uh", "uPh", "uPu", "PhPh", "PhPu", "PuPu")
LATER = (
    "xx", "xd", "dd", "xa", "xp", "da", "dp", "xPa", "xPp", "dPa", "dPp", "xPx", "xPd", "dPd",
    "PaPa", "PaPp", "PpPp", "PaPx", "PaPd", "PpPx", "PpPd", "PxPx", "PxPd", "PdPd",
)
LAST = ("xa", "xp", "da", "dp")


def split_name(name):
    parts, at = [], 0
    while at < len(name):
        size = 2 if name[at] == "P" else 1
        parts.append(name[at : at + size])
        at += size
    return parts


def first_scalars(gram_ref, entries):
    sums = gram_sums(gram_ref, entries)
    value = {name: sums(i) for i, name in enumerate(FIRST)}
    inverse = lax.rsqrt(value["uu"] + EPSILON)
    square = inverse * inverse
    named = [value[name] * square for name in FIRST]
    return (inverse,) + correction_scalars(*named)


def later_scalars(gram_ref, entries):
    sums = gram_sums(gram_ref, entries)
    value = {name: sums(i) for i, name in enumerate(LATER)}
    cosine, sine = rotation(value["xp"] + value["da"], value["dp"], value["xa"])
    cc, cs, ss = cosine * cosine, cosine * sine, sine * sine

    def turned(a, b, c, d):
        return cc * value[a] + cs * (value[b] + value[c]) + ss * value[d]

    named = (
        turned("xx", "xd", "xd", "dd"),
        turned("xa", "xp", "da", "dp"),
        turned("xPa", "xPp", "dPa", "dPp"),
        turned("xPx", "xPd", "xPd", "dPd"),
        turned("PaPa", "PaPp", "PaPp", "PpPp"),
        turned("PaPx", "PaPd", "PpPx", "PpPd"),
        turned("PxPx", "PxPd", "PxPd", "PdPd"),
    )
    return (cosine, sine) + correction_scalars(*named)


def apply_kernel(mode, entries, *refs):
    slot_ref, local_ref, mix_ref, right_ref, left_ref = refs[:5]
    refs = refs[5:]
    l = pl.program_id(0)
    if mode == "start":
        state_ref, send_ref, own_ref, first, second, fixed = refs
    elif mode == "first":
        gram_ref, u_ref, h_ref, weight_ref = refs[:4]
        x_out, a_out, d_out, send_ref, own_ref, first, second, fixed = refs[4:]
    else:
        gram_ref, x_ref, a_ref, d_ref, p_ref, weight_ref = refs[:6]
        x_out, a_out, d_out, send_ref, own_ref, first, second, fixed = refs[6:]

    @pl.when(l == 0)
    def _():
        own_ref[...] = jnp.zeros_like(own_ref)
        first[W * D * HALF :, :] = jnp.zeros((MIX * HALF - W * D * HALF, FOLD), F32)
        if mode != "start":
            scalars = first_scalars if mode == "first" else later_scalars
            for i, value in enumerate(scalars(gram_ref, entries)):
                fixed[i : i + 1, :] = jnp.broadcast_to(value, (1, FOLD))

    if mode == "start":
        vector = state_ref[0]
    else:
        if mode == "first":
            inverse, rho, along, norm = [fixed[i : i + 1, :] for i in range(4)]
            current = inverse * u_ref[0]
            applied = inverse * h_ref[0]
        else:
            cosine, sine, rho, along, norm = [fixed[i : i + 1, :] for i in range(5)]
            current = cosine * x_ref[0] + sine * d_ref[0]
            applied = cosine * a_ref[0] + sine * p_ref[0]
        vector = (weight_ref[0] * (applied - rho * current) - along * current) * norm
        x_out[0] = current
        a_out[0] = applied
        d_out[0] = vector

    right = jnp.concatenate(
        [spread(vector[s * HALF : (s + 1) * HALF]) for s in range(D)], axis=1
    ).astype(BF)
    step = GROUP * HALF
    for i in range(CLASSES):
        product = dot(right_ref[0, i * step : (i + 1) * step, :], right)
        for v in range(GROUP):
            for s in range(D):
                at = ((i * GROUP + v) * D + s) * HALF
                first[at : at + HALF, :] = product[v * HALF : (v + 1) * HALF, s * FOLD : (s + 1) * FOLD]
    mix_channels(mix_ref[...], first, second)
    for k in range(CLASSES):
        rows, blocks = [], []
        for w in range(k * GROUP, (k + 1) * GROUP):
            rows.append(second[w * TILE : (w + 1) * TILE, :].astype(BF))
            blocks.append(spread(left_ref[0, w * HALF : (w + 1) * HALF, :].astype(F32)).astype(BF))
        partial = dot(jnp.concatenate(rows, axis=1), jnp.concatenate(blocks, axis=0))
        slot = slot_ref[l * CLASSES + k]
        local = local_ref[l * CLASSES + k]

        @pl.when(slot >= 0)
        def _():
            send_ref[jnp.maximum(slot, 0)] = partial.astype(BF)

        @pl.when(slot < 0)
        def _():
            own_ref[local] = own_ref[local] + partial


def apply_operator(mode, entries, slots_total, slot, local, mix, right_env, left_env, gram, vectors):
    vector = pl.BlockSpec((1, TILE, FOLD), lambda l, *refs: (l, 0, 0))
    folded = pl.BlockSpec((1, ROWS, FOLD), lambda l, *refs: (l, 0, 0))
    whole = lambda shape: pl.BlockSpec(shape, lambda l, *refs: (0,) * len(shape))
    shape = jax.ShapeDtypeStruct((SEC_DEV, TILE, FOLD), F32)
    kept = 0 if mode == "start" else 3
    send = jax.ShapeDtypeStruct((slots_total, TILE, FOLD), BF)
    inputs = (mix, right_env, left_env) + (() if gram is None else (gram,)) + tuple(vectors)
    return pl.pallas_call(
        functools.partial(apply_kernel, mode, entries),
        out_shape=(shape,) * kept + (send, shape),
        grid_spec=pltpu.PrefetchScalarGridSpec(
            num_scalar_prefetch=2,
            grid=(SEC_DEV,),
            in_specs=[whole(mix.shape), folded, folded]
            + ([] if gram is None else [whole(gram.shape)])
            + [vector] * len(vectors),
            out_specs=(vector,) * kept + (whole(send.shape), whole(shape.shape)),
            scratch_shapes=[
                pltpu.VMEM((MIX * HALF, FOLD), F32),
                pltpu.VMEM((MIX * HALF, FOLD), F32),
                pltpu.VMEM((8, FOLD), F32),
            ],
        ),
        name="apply_" + mode,
        cost_estimate=pl.CostEstimate(flops=10**10, bytes_accessed=10**7, transcendentals=0),
    )(slot, local, *inputs)


def collect_kernel(names, *refs):
    take_ref, left_ref, right_ref = refs[:3]
    came_ref, own_ref = refs[3:5]
    symbols = sorted({part[-1] for name in names for part in split_name(name)} - {"h", "p"})
    weighted = any("P" in name for name in names)
    vectors = refs[5 : 5 + len(symbols)]
    at = 5 + len(symbols)
    weight_ref = None
    if weighted:
        weight_ref = refs[at]
        at += 1
    out_ref, gram_ref, sums = refs[at:]
    result = "h" if names is FIRST else "p"
    m = pl.program_id(0)

    @pl.when(m == 0)
    def _():
        sums[...] = jnp.zeros_like(sums)

    total = own_ref[0]
    for k in range(CLASSES):
        place = take_ref[k * SEC_DEV + m]
        part = came_ref[jnp.maximum(place, 0)].astype(F32)
        total = total + jnp.where(place >= 0, part, 0.0)
    total = live_mask(left_ref[m], [right_ref[m * D + t] for t in range(D)]) * total
    out_ref[0] = total
    size = 8
    totals = [jnp.zeros((size, FOLD), F32) for name in names]
    for i in range(TILE // size):
        rows = slice(i * size, (i + 1) * size)
        value = {symbol: ref[0, rows, :] for symbol, ref in zip(symbols, vectors)}
        value[result] = total[rows]
        if weighted:
            weight = weight_ref[0, rows, :]
            for symbol in list(value):
                value["P" + symbol] = weight * value[symbol]
        for n, name in enumerate(names):
            one, two = split_name(name)
            totals[n] = totals[n] + value[one] * value[two]
    for n in range(len(names)):
        sums[n] = sums[n] + totals[n]

    @pl.when(m == SEC_DEV - 1)
    def _():
        lane = lax.broadcasted_iota(jnp.int32, (8, FOLD), 1)
        packed = jnp.zeros((8, FOLD), F32)
        for n in range(len(names)):
            packed = jnp.where(lane == n, jnp.sum(sums[n], keepdims=True), packed)
        for g in range(gram_ref.shape[0]):
            gram_ref[g] = packed


def collect(names, groups, take, left_sizes, right_sizes, came, own, vectors, weight):
    vector = pl.BlockSpec((1, TILE, FOLD), lambda m, *refs: (m, 0, 0))
    whole = lambda shape: pl.BlockSpec(shape, lambda m, *refs: (0,) * len(shape))
    extra = () if weight is None else (weight,)
    gram = jax.ShapeDtypeStruct((groups, 8, FOLD), F32)
    return pl.pallas_call(
        functools.partial(collect_kernel, names),
        out_shape=(jax.ShapeDtypeStruct((SEC_DEV, TILE, FOLD), F32), gram),
        grid_spec=pltpu.PrefetchScalarGridSpec(
            num_scalar_prefetch=3,
            grid=(SEC_DEV,),
            in_specs=[whole(came.shape)] + [vector] * (1 + len(vectors) + len(extra)),
            out_specs=(vector, whole(gram.shape)),
            scratch_shapes=[pltpu.VMEM((len(names), 8, FOLD), F32)],
        ),
        name="collect",
        cost_estimate=pl.CostEstimate(flops=10**7, bytes_accessed=4 * 10**6, transcendentals=0),
    )(take, left_sizes, right_sizes, came, own, *vectors, *extra)


def finish_kernel(entries, gram_ref, x_ref, d_ref, state_ref, energy_ref, fixed):
    l = pl.program_id(0)

    @pl.when(l == 0)
    def _():
        sums = gram_sums(gram_ref, entries)
        xa, xp, da, dp = [sums(i) for i in range(4)]
        cosine, sine = rotation(xp + da, dp, xa)
        energy = cosine * cosine * xa + cosine * sine * (xp + da) + sine * sine * dp
        fixed[0:1, :] = jnp.broadcast_to(cosine, (1, FOLD))
        fixed[1:2, :] = jnp.broadcast_to(sine, (1, FOLD))
        energy_ref[...] = jnp.broadcast_to(energy, energy_ref.shape)

    final = fixed[0:1, :] * x_ref[0] + fixed[1:2, :] * d_ref[0]
    for i in range(D // 2):
        first = final[(2 * i) * HALF : (2 * i + 1) * HALF]
        second = final[(2 * i + 1) * HALF : (2 * i + 2) * HALF]
        state_ref[0, :, i * FOLD : (i + 1) * FOLD] = unfold_pair(first, second)


def finish(entries, gram, current, direction):
    vector = pl.BlockSpec((1, TILE, FOLD), lambda l: (l, 0, 0))
    return pl.pallas_call(
        functools.partial(finish_kernel, entries),
        grid=(SEC_DEV,),
        out_shape=(
            jax.ShapeDtypeStruct((SEC_DEV, B, D * B), F32),
            jax.ShapeDtypeStruct((8, FOLD), F32),
        ),
        in_specs=[pl.BlockSpec(gram.shape, lambda l: (0, 0, 0)), vector, vector],
        out_specs=(
            pl.BlockSpec((1, B, D * B), lambda l: (l, 0, 0)),
            pl.BlockSpec((8, FOLD), lambda l: (0, 0)),
        ),
        scratch_shapes=[pltpu.VMEM((8, FOLD), F32)],
        name="finish",
        cost_estimate=pl.CostEstimate(flops=10**6, bytes_accessed=2 * 10**6, transcendentals=0),
    )(gram, current, direction)


def exchange(blocks):
    return lax.all_to_all(blocks, "sec", 0, 0, tiled=True)


def on_device(
    left_environment,
    right_environment,
    site_previous,
    state_start,
    preconditioner,
    channel_tensor,
    channel_mask,
    sector_shift,
    left_sizes,
    right_sizes,
):
    groups = lax.axis_size("sec")
    my_group = lax.axis_index("sec")
    offset = my_group * SEC_DEV
    slots = (PAIRS + groups - 1) // groups
    entries = float(SEC_DEV * B * D * B * groups)
    my_left = lax.dynamic_slice_in_dim(left_sizes, offset, SEC_DEV, 0)
    my_right = lax.dynamic_slice_in_dim(right_sizes, offset, SEC_DEV, 0).reshape(SEC_DEV * D)
    position = lax.axis_index("seg")
    last = lax.axis_size("seg") - 1

    came_right = passed_along(right_environment[0], "seg", -1)
    right_used = jnp.where(position == last, right_environment[0], came_right)

    slot, local, take, site_send = route(my_group[None], sector_shift, site_previous[0], groups, slots)
    site_came = exchange(site_send).reshape(groups * slots, B, D * B)
    mix = channel_tensor * channel_mask.astype(BF)[:, None, :, None]
    mix = jnp.pad(mix.reshape(W * D, W * D), ((0, MIX - W * D), (0, MIX - W * D)))

    own_left = fold_environment(left_environment[0])
    fresh = build_environment(slot, local, own_left, site_previous[0], site_came, mix)
    handed = passed_along(fresh, "seg", 1)
    left_env = jnp.where(position == 0, own_left, handed)
    right_env = fold_environment(right_used)
    start, weight = fold_state(my_left, my_right, state_start[0], preconditioner[0])

    apply = functools.partial(
        apply_operator, entries=entries, slots_total=groups * slots, slot=slot, local=local, mix=mix,
        right_env=right_env, left_env=left_env,
    )

    def gather(names, send, own, vectors, weight):
        came = exchange(send.reshape(groups, slots, TILE, FOLD)).reshape(groups * slots, TILE, FOLD)
        result, gram = collect(names, groups, take, my_left, my_right, came, own, vectors, weight)
        return result, exchange(gram)

    send, own = apply("start", gram=None, vectors=(start,))
    product, gram = gather(FIRST, send, own, (start,), weight)
    current, applied, direction, send, own = apply("first", gram=gram, vectors=(start, product, weight))
    product, gram = gather(LATER, send, own, (applied, direction, current), weight)
    current, applied, direction, send, own = apply(
        "later", gram=gram, vectors=(current, applied, direction, product, weight)
    )
    product, gram = gather(LAST, send, own, (applied, direction, current), None)
    state, energy = finish(entries, gram, current, direction)
    return (state[None], energy[0, :1])


def solution(mesh):
    in_specs = (
        P("seg", "sec", None, None),
        P("seg", "sec", None, None),
        P("seg", "sec", None, None),
        P("seg", "sec", None, None),
        P("seg", "sec", None, None),
        P(),
        P(),
        P(),
        P(),
        P(),
    )
    out_specs = (P("seg", "sec", None, None), P("seg"))
    return jax.shard_map(
        on_device, mesh=mesh, in_specs=in_specs, out_specs=out_specs, check_vma=False
    )
```

time: 1340 us -> 351 us (0.26)
  matrix products: 388 us -> 0 us
  waiting for transfers between devices: 304 us -> 18.6 us
  blocking collectives: 381 us -> 110 us
  Pallas kernels: 0 us -> 195 us
  local copies, waits for them, and re-layouts: 197 us -> 5.84 us
  between operations: 26.5 us -> 0.78 us
  other arithmetic: 30.9 us -> 6.4 us
    dot_general x23 -> x0, matrix products: 388 us -> none  [the longest x3 141 us: apply_operator(): jnp.einsum('wtvs,lasvc->lwatc', channel_mix, right_product, preferred_ele...]
    psum x10 -> x0, blocking collectives: 381 us -> none  [the longest x3 111 us: rayleigh(): return lax.psum(jnp.sum(vector * result), 'sec') / total_entries]
    psum x3 -> x0, waiting for transfers between devices: 303 us -> none  [apply_operator(): lax.psum(every_row.astype(jnp.bfloat16), 'sec').astype(jnp.float32)]
    pallas_call x0 -> x12, Pallas kernels: none -> 195 us  [the longest x3 109 us: apply_operator(): pl.pallas_call(functools.partial(apply_kernel, mode, entries), out_shape=...]
    all_to_all x0 -> x6, blocking collectives: none -> 110 us  [exchange(): return lax.all_to_all(blocks, 'sec', 0, 0, tiled=True)]
    convert_element_type x4 -> x0, local copies, waits for them, and re-layouts: 59.3 us -> none  [the longest x3 54.7 us: apply_operator(): mixed_product = jnp.einsum('wtvs,lasvc->lwatc', channel_mix, right_produc...]
    reshape x9 -> x2, local copies, waits for them, and re-layouts: 55.6 us -> 2.3 us  [the longest x1 1.71 us: on_device(): mix.reshape(W * D, W * D)]
    dot_general x3 -> x0, local copies, waits for them, and re-layouts: 28.6 us -> none  [apply_operator(): jnp.einsum('lpkja,lkjatc->lkptc', left_split, grouped, preferred_element_...]
  transfers between devices with their start and end apart: 6 -> 3, of which waited for: 3 -> 2; matrix products, arithmetic and copies ran while one was open for 13% -> 2% of each run, Pallas kernels for 0% -> 14%
where the time goes in v1:
time: 351 us; the launch traced here: 348 us
  Pallas kernels  195 us (56%)
  blocking collectives  110 us (31%)
  waiting for transfers between devices  18.6 us (5%)
  starting transfers between devices  11.9 us (3%)
  other arithmetic  6.4 us (2%)
  local copies, waits for them, and re-layouts  5.84 us (2%)
    all_to_all x6, blocking collectives, exchange(): return lax.all_to_all(blocks, 'sec', 0, 0, tiled=True)  110 us
    pallas_call x3, Pallas kernels, apply_operator(): pl.pallas_call(functools.partial(apply_kernel, mode, entries), out_shape=...  109 us
    pallas_call x1, Pallas kernels, build_environment(): pl.pallas_call(build_kernel, out_shape=jax.ShapeDtypeStruct((SEC_DEV, ROW...  29.2 us
    pallas_call x3, Pallas kernels, collect(): pl.pallas_call(functools.partial(collect_kernel, names), out_shape=(jax.S...  21.4 us
    pallas_call x2, Pallas kernels, fold_environment(): pl.pallas_call(fold_environment_kernel, grid=(SEC_DEV,), out_shape=jax.Sh...  14.1 us
    all_to_all x1, waiting for transfers between devices, exchange(): return lax.all_to_all(blocks, 'sec', 0, 0, tiled=True)  12.3 us
    pallas_call x1, Pallas kernels, route(): pl.pallas_call(route_kernel, out_shape=(jax.ShapeDtypeStruct((PAIRS,), jn...  9.3 us
    all_to_all x1, starting transfers between devices, exchange(): return lax.all_to_all(blocks, 'sec', 0, 0, tiled=True)  8.11 us
  transfers between devices with their start and end apart: 3, of which 2 were waited for; matrix products, arithmetic and copies ran while one was open for 2% of the time, Pallas kernels for 14%

profile of v1, /device:TPU:2, one launch (start us, length us, event | category | flops | bytes accessed | tf_op | source)
XLA Modules:
  0.0 347.9 jit_solution(11750473151323136424)
XLA Ops:
  0.7 9.3 %route.1 = (s32[40]{0:T(128)}, s32[40]{0:T(128)}, s32[40]{0:T(128)}, bf16[16,3,64,256]{3,2,1,0:T(8,128)(2,1)}) custom-call(s32[1]{0:T(128)} %bitcast.me_ref, s32[5,128]{1,0:T(8,128)} %shift_ref.1, bf16[8,64,256]{2,1,0:T(8,128)(2,1)} %bitcast.26), custom_call_target="tpu_custom_call" | custom-call | tf_op jit(solution)/shard_map/route/pallas_call | solution.py:126
  10.0 8.1 %all-to-all-start = ((bf16[16,3,64,256]{3,2,1,0:T(8,128)(2,1)}), bf16[16,3,64,256]{3,2,1,0:T(8,128)(2,1)}, u32[]{:S(2)}, u32[]{:S(2)}) async-start(bf16[16,3,64,256]{3,2,1,0:T(8,128)(2,1)} %get-tuple-element.30), calls=%async_computation | async-start | bytes 3145728 | tf_op jit(solution)/shard_map/all_to_all | solution.py:561
  18.1 1.9 collective-permute-start
  22.8 7.0 %fold_environment.3.env_ref = bf16[8,960,128]{2,1,0:T(8,128)(2,1)} custom-call(bf16[8,64,1920]{2,1,0:T(8,128)(2,1)} %bitcast.19), custom_call_target="tpu_custom_call" | custom-call | bytes 3932160 | tf_op jit(solution)/shard_map/fold_environment/pallas_call | solution.py:150
  30.4 12.3 %all-to-all-done = bf16[16,3,64,256]{3,2,1,0:T(8,128)(2,1)} async-done(((bf16[16,3,64,256]{3,2,1,0:T(8,128)(2,1)}), bf16[16,3,64,256]{3,2,1,0:T(8,128)(2,1)}, u32[]{:S(2)}, u32[]{:S(2)}) %all-to-all-start) | async-done | bytes 1572896 | tf_op jit(solution)/shard_map/all_to_all | solution.py:561
  42.7 29.2 %build_environment.1 = bf16[8,960,128]{2,1,0:T(8,128)(2,1)} custom-call(s32[40]{0:T(128)} %get-tuple-element.28.slot_ref.refs_0_, s32[40]{0:T(128)} %get-tuple-element.29.local_ref.refs_1_, bf16[8,960,128]{2,1,0:T(8,128)(2,1)} %fold_environment.3.env_ref, bf16[8,64,256]{2,1,0:T(8,128)(2,1)} %bitcast.27, bf16[48,64,256]{2,1,0:T(8,128)(2,1)} %bitcast.4.came_ref, ...), custom_call_target="tpu_custom_call" | custom-call | flops 10000000000 | bytes 10000000 | tf_op jit(solution)/shard_map/build_environment/pallas_call | solution.py:257
  75.2 6.3 %fold_state.1 = (f32[8,128,128]{2,1,0:T(8,128)}, f32[8,128,128]{2,1,0:T(8,128)}) custom-call(s32[8]{0:T(128)} %dynamic_slice.6.left_ref.refs_1_, s32[32]{0:T(128)} %reshape.32.right_ref.refs_2_, f32[8,64,256]{2,1,0:T(8,128)} %bitcast.24, f32[8,64,256]{2,1,0:T(8,128)} %bitcast.25), custom_call_target="tpu_custom_call" | custom-call | bytes 2097152 | tf_op jit(solution)/shard_map/fold_state/pallas_call | solution.py:186
  81.5 3.3 broadcast_select_fusion.1.in_ref
  84.8 7.1 %fold_environment.2.refs_3_ = bf16[8,960,128]{2,1,0:T(8,128)(2,1)} custom-call(bf16[8,64,1920]{2,1,0:T(8,128)(2,1)} %broadcast_select_fusion.1.in_ref), custom_call_target="tpu_custom_call" | custom-call | bytes 3932160 | tf_op jit(solution)/shard_map/fold_environment/pallas_call | solution.py:150
  91.9 6.3 %collective-permute-done.1 = bf16[8,960,128]{2,1,0:T(8,128)(2,1)} collective-permute-done((bf16[8,960,128]{2,1,0:T(8,128)(2,1)}, bf16[8,960,128]{2,1,0:T(8,128)(2,1)}, u32[]{:S(2)}, u32[]{:S(2)}) %collective-permute-start.1) | collective-permute-done | bytes 1966112 | tf_op jit(solution)/shard_map/ppermute | solution.py:30
  98.2 3.0 broadcast_select_fusion.refs_4_
  101.2 35.7 %apply_start.1 = (bf16[48,128,128]{2,1,0:T(8,128)(2,1)}, f32[8,128,128]{2,1,0:T(8,128)}) custom-call(s32[40]{0:T(128)} %get-tuple-element.28.slot_ref.refs_0_, s32[40]{0:T(128)} %get-tuple-element.29.local_ref.refs_1_, bf16[128,128]{1,0:T(8,128)(2,1)} %pad.4.mix_ref.refs_2_, bf16[8,960,128]{2,1,0:T(8,128)(2,1)} %fold_environment.2.refs_3_, ...), custom_call_target="tpu_custom_call" | custom-call | flops 10000000000 | bytes 10000000 | tf_op jit(solution)/shard_map/apply_start/pallas_call | solution.py:427
  136.9 26.7 %all_to_all.35 = bf16[16,3,128,128]{3,2,1,0:T(8,128)(2,1)} all-to-all(bf16[16,3,128,128]{3,2,1,0:T(8,128)(2,1)} %bitcast.23), channel_id=1, replica_groups=mesh['seg'=8,'sec'=16] {'sec'}, dimensions={0} | all-to-all | bytes 3145728 | tf_op jit(solution)/shard_map/all_to_all | solution.py:561
  163.7 6.9 %collect.3 = (f32[8,128,128]{2,1,0:T(8,128)}, f32[16,8,128]{2,1,0:T(8,128)}) custom-call(s32[40]{0:T(128)} %get-tuple-element.27.refs_0_, s32[8]{0:T(128)} %dynamic_slice.6.left_ref.refs_1_, s32[32]{0:T(128)} %reshape.32.right_ref.refs_2_, bf16[48,128,128]{2,1,0:T(8,128)(2,1)} %bitcast.17, f32[8,128,128]{2,1,0:T(8,128)} %get-tuple-element.33.refs_4_, ...), custom_call_target="tpu_custom_call" | custom-call | flops 10000000 | bytes 4000000 | tf_op jit(solution)/shard_map/collect/pallas_call | solution.py:505
  170.6 12.0 %all_to_all.36.refs_5_ = f32[16,8,128]{2,1,0:T(8,128)} all-to-all(f32[16,8,128]{2,1,0:T(8,128)} %get-tuple-element.35), channel_id=1, replica_groups=mesh['seg'=8,'sec'=16] {'sec'}, dimensions={0} | all-to-all | bytes 131072 | tf_op jit(solution)/shard_map/all_to_all | solution.py:561
  182.5 36.3 %apply_first.1 = (f32[8,128,128]{2,1,0:T(8,128)}, f32[8,128,128]{2,1,0:T(8,128)}, f32[8,128,128]{2,1,0:T(8,128)}, bf16[48,128,128]{2,1,0:T(8,128)(2,1)}, f32[8,128,128]{2,1,0:T(8,128)}) custom-call(s32[40]{0:T(128)} %get-tuple-element.28.slot_ref.refs_0_, s32[40]{0:T(128)} %get-tuple-element.29.local_ref.refs_1_, bf16[128,128]{1,0:T(8,128)(2,1)} %pad.4.mix_ref.refs_2_, ...), custom_call_target="tpu_custom_call" | custom-call | flops 10000000000 | bytes 10000000 | tf_op jit(solution)/shard_map/apply_first/pallas_call | solution.py:427
  218.8 24.9 %all_to_all.37 = bf16[16,3,128,128]{3,2,1,0:T(8,128)(2,1)} all-to-all(bf16[16,3,128,128]{3,2,1,0:T(8,128)(2,1)} %bitcast.22), channel_id=1, replica_groups=mesh['seg'=8,'sec'=16] {'sec'}, dimensions={0} | all-to-all | bytes 3145728 | tf_op jit(solution)/shard_map/all_to_all | solution.py:561
  243.7 7.5 %collect.4 = (f32[8,128,128]{2,1,0:T(8,128)}, f32[16,8,128]{2,1,0:T(8,128)}) custom-call(s32[40]{0:T(128)} %get-tuple-element.27.refs_0_, s32[8]{0:T(128)} %dynamic_slice.6.left_ref.refs_1_, s32[32]{0:T(128)} %reshape.32.right_ref.refs_2_, bf16[48,128,128]{2,1,0:T(8,128)(2,1)} %bitcast.18, f32[8,128,128]{2,1,0:T(8,128)} %get-tuple-element.38.refs_4_, ...), custom_call_target="tpu_custom_call" | custom-call | flops 10000000 | bytes 4000000 | tf_op jit(solution)/shard_map/collect/pallas_call | solution.py:505
  251.2 11.8 %all_to_all.38.refs_5_ = f32[16,8,128]{2,1,0:T(8,128)} all-to-all(f32[16,8,128]{2,1,0:T(8,128)} %get-tuple-element.42), channel_id=1, replica_groups=mesh['seg'=8,'sec'=16] {'sec'}, dimensions={0} | all-to-all | bytes 131072 | tf_op jit(solution)/shard_map/all_to_all | solution.py:561
  263.0 36.5 %apply_later.1 = (f32[8,128,128]{2,1,0:T(8,128)}, f32[8,128,128]{2,1,0:T(8,128)}, f32[8,128,128]{2,1,0:T(8,128)}, bf16[48,128,128]{2,1,0:T(8,128)(2,1)}, f32[8,128,128]{2,1,0:T(8,128)}) custom-call(s32[40]{0:T(128)} %get-tuple-element.28.slot_ref.refs_0_, s32[40]{0:T(128)} %get-tuple-element.29.local_ref.refs_1_, bf16[128,128]{1,0:T(8,128)(2,1)} %pad.4.mix_ref.refs_2_, ...), custom_call_target="tpu_custom_call" | custom-call | flops 10000000000 | bytes 10000000 | tf_op jit(solution)/shard_map/apply_later/pallas_call | solution.py:427
  299.5 22.8 %all_to_all.39 = bf16[16,3,128,128]{3,2,1,0:T(8,128)(2,1)} all-to-all(bf16[16,3,128,128]{3,2,1,0:T(8,128)(2,1)} %bitcast.21), channel_id=1, replica_groups=mesh['seg'=8,'sec'=16] {'sec'}, dimensions={0} | all-to-all | bytes 3145728 | tf_op jit(solution)/shard_map/all_to_all | solution.py:561
  322.3 7.0 %collect.5 = (f32[8,128,128]{2,1,0:T(8,128)}, f32[16,8,128]{2,1,0:T(8,128)}) custom-call(s32[40]{0:T(128)} %get-tuple-element.27.refs_0_, s32[8]{0:T(128)} %dynamic_slice.6.left_ref.refs_1_, s32[32]{0:T(128)} %reshape.32.right_ref.refs_2_, bf16[48,128,128]{2,1,0:T(8,128)(2,1)} %bitcast.16, f32[8,128,128]{2,1,0:T(8,128)} %get-tuple-element.45.refs_4_, ...), custom_call_target="tpu_custom_call" | custom-call | flops 10000000 | bytes 4000000 | tf_op jit(solution)/shard_map/collect/pallas_call | solution.py:505
  329.2 11.8 %all_to_all.40.gram_ref = f32[16,8,128]{2,1,0:T(8,128)} all-to-all(f32[16,8,128]{2,1,0:T(8,128)} %get-tuple-element.49), channel_id=1, replica_groups=mesh['seg'=8,'sec'=16] {'sec'}, dimensions={0} | all-to-all | bytes 131072 | tf_op jit(solution)/shard_map/all_to_all | solution.py:561
  341.0 5.7 %finish.1 = (f32[8,64,256]{2,1,0:T(8,128)}, f32[8,128]{1,0:T(8,128)}) custom-call(f32[16,8,128]{2,1,0:T(8,128)} %all_to_all.40.gram_ref, f32[8,128,128]{2,1,0:T(8,128)} %get-tuple-element.48.refs_7_.x_ref, f32[8,128,128]{2,1,0:T(8,128)} %get-tuple-element.47.refs_6_.d_ref), custom_call_target="tpu_custom_call" | custom-call | flops 1000000 | bytes 2000000 | tf_op jit(solution)/shard_map/finish/pallas_call | solution.py:542
  (24 shorter events, 7.8 us)
Async XLA Ops:
  0.6 73.8 %copy-start = (s32[128,4]{0,1:T(4,128)S(1)}, s32[128,4]{0,1:T(4,128)}, u32[]{:S(2)}) copy-start(s32[128,4]{0,1:T(4,128)} %param.19) | copy-start | bytes 6148
  0.6 17.5 %copy-start.2 = (bf16[1,8,64,1920]{3,2,1,0:T(8,128)(2,1)S(1)}, bf16[1,8,64,1920]{3,2,1,0:T(8,128)(2,1)}, u32[]{:S(2)}) copy-start(bf16[1,8,64,1920]{3,2,1,0:T(8,128)(2,1)} %param.11) | copy-start | bytes 5898244
  0.7 19.4 %copy-start.4 = (s32[30,30]{1,0:T(8,128)S(1)}, s32[30,30]{1,0:T(8,128)}, u32[]{:S(2)}) copy-start(s32[30,30]{1,0:T(8,128)} %param.16) | copy-start | bytes 10804
  0.7 19.4 %copy-start.3 = (bf16[30,4,30,4]{2,3,1,0:T(4,128)(2,1)S(1)}, bf16[30,4,30,4]{2,3,1,0:T(4,128)(2,1)}, u32[]{:S(2)}) copy-start(bf16[30,4,30,4]{2,3,1,0:T(4,128)(2,1)} %param.15) | copy-start | bytes 86404
  10.0 32.7 %all-to-all-start = ((bf16[16,3,64,256]{3,2,1,0:T(8,128)(2,1)}), bf16[16,3,64,256]{3,2,1,0:T(8,128)(2,1)}, u32[]{:S(2)}, u32[]{:S(2)}) async-start(bf16[16,3,64,256]{3,2,1,0:T(8,128)(2,1)} %get-tuple-element.30), calls=%async_computation | async-start | bytes 3145728 | tf_op jit(solution)/shard_map/all_to_all | solution.py:561
  18.1 63.4 %collective-permute-start = (bf16[8,64,1920]{2,1,0:T(8,128)(2,1)S(1)}, bf16[8,64,1920]{2,1,0:T(8,128)(2,1)}, u32[]{:S(2)}, u32[]{:S(2)}) collective-permute-start(bf16[8,64,1920]{2,1,0:T(8,128)(2,1)S(1)} %bitcast.20), channel_id=1, source_target_pairs={{16,0},{32,16},{48,32},{64,48},{80,64},{96,80},{112,96},{17,1},{33... | collective-permute-start | bytes 5898248 | tf_op jit(solution)/shard_map/ppermute | solution.py:30
  42.7 31.2 %copy-start.5 = (s32[128]{0:T(128)S(1)}, s32[128]{0:T(128)}, u32[]{:S(2)}) copy-start(s32[128]{0:T(128)} %param.18) | copy-start | bytes 1540
  71.9 26.3 %collective-permute-start.1 = (bf16[8,960,128]{2,1,0:T(8,128)(2,1)}, bf16[8,960,128]{2,1,0:T(8,128)(2,1)}, u32[]{:S(2)}, u32[]{:S(2)}) collective-permute-start(bf16[8,960,128]{2,1,0:T(8,128)(2,1)} %build_environment.1), channel_id=1, source_target_pairs={{0,16},{16,32},{32,48},{48,64},{64,80},{80,96},{96,112},{1,17},{17... | collective-permute-start | bytes 5898248 | tf_op jit(solution)/shard_map/ppermute | solution.py:30
  84.8 13.4 %copy-start.1 = (bf16[8,960,128]{2,1,0:T(8,128)(2,1)S(1)}, bf16[8,960,128]{2,1,0:T(8,128)(2,1)}, u32[]{:S(2)}) copy-start(bf16[8,960,128]{2,1,0:T(8,128)(2,1)} %fold_environment.3.env_ref) | copy-start | bytes 5898244

commit v2 on v1

--- a/solution.py
+++ b/solution.py
@@ -19,6 +19,7 @@
 ROWS = W * HALF
 TILE = D * HALF
 MIX = 128
+PITCH = 33
 EPSILON = 1e-06
 BF = jnp.bfloat16
 F32 = jnp.float32
@@ -199,10 +200,16 @@
 
 def mix_channels(mix, first, second):
     for j in range(0, HALF, 2):
-        parts = [first[pl.ds(j + i, MIX, stride=HALF), :].astype(BF) for i in range(2)]
+        parts = [first[pl.ds(j + i, MIX, stride=PITCH), :].astype(BF) for i in range(2)]
         mixed = dot(mix, jnp.concatenate(parts, axis=1))
         for i in range(2):
-            second[pl.ds(j + i, MIX, stride=HALF), :] = mixed[:, i * FOLD : (i + 1) * FOLD]
+            second[pl.ds(j + i, MIX, stride=PITCH), :] = mixed[:, i * FOLD : (i + 1) * FOLD]
+
+
+def mixed_rows(ref, x):
+    return jnp.concatenate(
+        [ref[(x * D + y) * PITCH : (x * D + y) * PITCH + HALF, :].astype(BF) for y in range(D)], axis=0
+    )
 
 
 def build_kernel(slot_ref, local_ref, env_ref, own_ref, came_ref, mix_ref, out_ref, first, second):
@@ -210,7 +217,7 @@
 
     @pl.when(l == 0)
     def _():
-        first[W * D * HALF :, :] = jnp.zeros((MIX * HALF - W * D * HALF, FOLD), F32)
+        first[W * D * PITCH :, :] = jnp.zeros(((MIX - W * D) * PITCH, FOLD), F32)
 
     mix_turned = mix_ref[...].astype(F32).T.astype(BF)
     for k in range(CLASSES):
@@ -225,7 +232,7 @@
         joined = dot(left, right)
         for j in range(GROUP):
             for t in range(D):
-                at = ((k * GROUP + j) * D + t) * HALF
+                at = ((k * GROUP + j) * D + t) * PITCH
                 first[at : at + HALF, :] = joined[j * HALF : (j + 1) * HALF, t * FOLD : (t + 1) * FOLD]
     mix_channels(mix_turned, first, second)
     own = own_ref[l]
@@ -240,7 +247,7 @@
     low = low_lanes(B)
     for v in range(0, W, 2):
         right = jnp.concatenate(
-            [second[(v + i) * TILE : (v + i + 1) * TILE, :].astype(BF) for i in range(2)], axis=1
+            [mixed_rows(second, v + i) for i in range(2)], axis=1
         )
         product = dot(turned, right)
         for i in range(2):
@@ -262,7 +269,7 @@
             grid=(SEC_DEV,),
             in_specs=[folded, whole(site.shape), whole(came.shape), whole(mix.shape)],
             out_specs=folded,
-            scratch_shapes=[pltpu.VMEM((MIX * HALF, FOLD), F32), pltpu.VMEM((MIX * HALF, FOLD), F32)],
+            scratch_shapes=[pltpu.VMEM((MIX * PITCH, FOLD), F32), pltpu.VMEM((MIX * PITCH, FOLD), F32)],
         ),
         name="build_environment",
         cost_estimate=pl.CostEstimate(flops=10**10, bytes_accessed=10**7, transcendentals=0),
@@ -365,7 +372,7 @@
     @pl.when(l == 0)
     def _():
         own_ref[...] = jnp.zeros_like(own_ref)
-        first[W * D * HALF :, :] = jnp.zeros((MIX * HALF - W * D * HALF, FOLD), F32)
+        first[W * D * PITCH :, :] = jnp.zeros(((MIX - W * D) * PITCH, FOLD), F32)
         if mode != "start":
             scalars = first_scalars if mode == "first" else later_scalars
             for i, value in enumerate(scalars(gram_ref, entries)):
@@ -395,13 +402,13 @@
         product = dot(right_ref[0, i * step : (i + 1) * step, :], right)
         for v in range(GROUP):
             for s in range(D):
-                at = ((i * GROUP + v) * D + s) * HALF
+                at = ((i * GROUP + v) * D + s) * PITCH
                 first[at : at + HALF, :] = product[v * HALF : (v + 1) * HALF, s * FOLD : (s + 1) * FOLD]
     mix_channels(mix_ref[...], first, second)
     for k in range(CLASSES):
         rows, blocks = [], []
         for w in range(k * GROUP, (k + 1) * GROUP):
-            rows.append(second[w * TILE : (w + 1) * TILE, :].astype(BF))
+            rows.append(mixed_rows(second, w))
             blocks.append(spread(left_ref[0, w * HALF : (w + 1) * HALF, :].astype(F32)).astype(BF))
         partial = dot(jnp.concatenate(rows, axis=1), jnp.concatenate(blocks, axis=0))
         slot = slot_ref[l * CLASSES + k]
@@ -435,8 +442,8 @@
             + [vector] * len(vectors),
             out_specs=(vector,) * kept + (whole(send.shape), whole(shape.shape)),
             scratch_shapes=[
-                pltpu.VMEM((MIX * HALF, FOLD), F32),
-                pltpu.VMEM((MIX * HALF, FOLD), F32),
+                pltpu.VMEM((MIX * PITCH, FOLD), F32),
+                pltpu.VMEM((MIX * PITCH, FOLD), F32),
                 pltpu.VMEM((8, FOLD), F32),
             ],
         ),

time: 351 us -> 292 us (0.83)
  Pallas kernels: 195 us -> 136 us
    pallas_call x3, Pallas kernels: 109 us -> 65 us  [apply_operator(): pl.pallas_call(functools.partial(apply_kernel, mode, entries), out_shape=...]
    pallas_call x1, Pallas kernels: 29.2 us -> 14.5 us  [build_environment(): pl.pallas_call(build_kernel, out_shape=jax.ShapeDtypeStruct((SEC_DEV, ROW...]
  transfers between devices with their start and end apart: 3 -> 3, of which waited for: 2 -> 2; matrix products, arithmetic and copies ran while one was open for 2% -> 3% of each run, Pallas kernels for 14% -> 12%
where the time goes in v2:
time: 292 us; the launch traced here: 290 us
  Pallas kernels  136 us (47%)
  blocking collectives  110 us (38%)
  waiting for transfers between devices  18.6 us (6%)
  starting transfers between devices  11.9 us (4%)
  other arithmetic  6.4 us (2%)
  local copies, waits for them, and re-layouts  5.84 us (2%)
    all_to_all x6, blocking collectives, exchange(): return lax.all_to_all(blocks, 'sec', 0, 0, tiled=True)  110 us
    pallas_call x3, Pallas kernels, apply_operator(): pl.pallas_call(functools.partial(apply_kernel, mode, entries), out_shape=...  65 us
    pallas_call x3, Pallas kernels, collect(): pl.pallas_call(functools.partial(collect_kernel, names), out_shape=(jax.S...  21.4 us
    pallas_call x1, Pallas kernels, build_environment(): pl.pallas_call(build_kernel, out_shape=jax.ShapeDtypeStruct((SEC_DEV, ROW...  14.5 us
    pallas_call x2, Pallas kernels, fold_environment(): pl.pallas_call(fold_environment_kernel, grid=(SEC_DEV,), out_shape=jax.Sh...  14.1 us
    all_to_all x1, waiting for transfers between devices, exchange(): return lax.all_to_all(blocks, 'sec', 0, 0, tiled=True)  12.3 us
    pallas_call x1, Pallas kernels, route(): pl.pallas_call(route_kernel, out_shape=(jax.ShapeDtypeStruct((PAIRS,), jn...  9.3 us
    all_to_all x1, starting transfers between devices, exchange(): return lax.all_to_all(blocks, 'sec', 0, 0, tiled=True)  8.11 us
  transfers between devices with their start and end apart: 3, of which 2 were waited for; matrix products, arithmetic and copies ran while one was open for 3% of the time, Pallas kernels for 12%

profile of v2, /device:TPU:2, one launch (start us, length us, event | category | flops | bytes accessed | tf_op | source)
XLA Modules:
  0.0 289.5 jit_solution(14857325985754400361)
XLA Ops:
  0.7 9.3 %route.1 = (s32[40]{0:T(128)}, s32[40]{0:T(128)}, s32[40]{0:T(128)}, bf16[16,3,64,256]{3,2,1,0:T(8,128)(2,1)}) custom-call(s32[1]{0:T(128)} %bitcast.me_ref, s32[5,128]{1,0:T(8,128)} %shift_ref.1, bf16[8,64,256]{2,1,0:T(8,128)(2,1)} %bitcast.26), custom_call_target="tpu_custom_call" | custom-call | tf_op jit(solution)/shard_map/route/pallas_call | solution.py:127
  10.0 8.1 %all-to-all-start = ((bf16[16,3,64,256]{3,2,1,0:T(8,128)(2,1)}), bf16[16,3,64,256]{3,2,1,0:T(8,128)(2,1)}, u32[]{:S(2)}, u32[]{:S(2)}) async-start(bf16[16,3,64,256]{3,2,1,0:T(8,128)(2,1)} %get-tuple-element.30), calls=%async_computation | async-start | bytes 3145728 | tf_op jit(solution)/shard_map/all_to_all | solution.py:568
  18.1 1.9 collective-permute-start
  22.8 7.0 %fold_environment.3.env_ref = bf16[8,960,128]{2,1,0:T(8,128)(2,1)} custom-call(bf16[8,64,1920]{2,1,0:T(8,128)(2,1)} %bitcast.19), custom_call_target="tpu_custom_call" | custom-call | bytes 3932160 | tf_op jit(solution)/shard_map/fold_environment/pallas_call | solution.py:151
  30.4 12.3 %all-to-all-done = bf16[16,3,64,256]{3,2,1,0:T(8,128)(2,1)} async-done(((bf16[16,3,64,256]{3,2,1,0:T(8,128)(2,1)}), bf16[16,3,64,256]{3,2,1,0:T(8,128)(2,1)}, u32[]{:S(2)}, u32[]{:S(2)}) %all-to-all-start) | async-done | bytes 1572896 | tf_op jit(solution)/shard_map/all_to_all | solution.py:568
  42.7 14.5 %build_environment.1 = bf16[8,960,128]{2,1,0:T(8,128)(2,1)} custom-call(s32[40]{0:T(128)} %get-tuple-element.28.slot_ref.refs_0_, s32[40]{0:T(128)} %get-tuple-element.29.local_ref.refs_1_, bf16[8,960,128]{2,1,0:T(8,128)(2,1)} %fold_environment.3.env_ref, bf16[8,64,256]{2,1,0:T(8,128)(2,1)} %bitcast.27, bf16[48,64,256]{2,1,0:T(8,128)(2,1)} %bitcast.4.came_ref, ...), custom_call_target="tpu_custom_call" | custom-call | flops 10000000000 | bytes 10000000 | tf_op jit(solution)/shard_map/build_environment/pallas_call | solution.py:264
  60.5 6.3 %fold_state.1 = (f32[8,128,128]{2,1,0:T(8,128)}, f32[8,128,128]{2,1,0:T(8,128)}) custom-call(s32[8]{0:T(128)} %dynamic_slice.6.left_ref.refs_1_, s32[32]{0:T(128)} %reshape.32.right_ref.refs_2_, f32[8,64,256]{2,1,0:T(8,128)} %bitcast.24, f32[8,64,256]{2,1,0:T(8,128)} %bitcast.25), custom_call_target="tpu_custom_call" | custom-call | bytes 2097152 | tf_op jit(solution)/shard_map/fold_state/pallas_call | solution.py:187
  66.8 3.3 %broadcast_select_fusion.1.in_ref = bf16[8,64,1920]{2,1,0:T(8,128)(2,1)} fusion(bf16[8,64,1920]{2,1,0:T(8,128)(2,1)} %collective-permute-done, pred[]{:T(512)S(6)} %eq.6, bf16[1,8,64,1920]{3,2,1,0:T(8,128)(2,1)S(1)} %copy-done.2), kind=kLoop, calls=%fused_computation.1 | loop fusion | flops 983040 | bytes 5898241 | tf_op jit(solution)/shard_map/jit(_where)/select_n | solution.py:594
  70.0 7.1 %fold_environment.2.refs_3_ = bf16[8,960,128]{2,1,0:T(8,128)(2,1)} custom-call(bf16[8,64,1920]{2,1,0:T(8,128)(2,1)} %broadcast_select_fusion.1.in_ref), custom_call_target="tpu_custom_call" | custom-call | bytes 3932160 | tf_op jit(solution)/shard_map/fold_environment/pallas_call | solution.py:151
  77.2 6.3 %collective-permute-done.1 = bf16[8,960,128]{2,1,0:T(8,128)(2,1)} collective-permute-done((bf16[8,960,128]{2,1,0:T(8,128)(2,1)}, bf16[8,960,128]{2,1,0:T(8,128)(2,1)}, u32[]{:S(2)}, u32[]{:S(2)}) %collective-permute-start.1) | collective-permute-done | bytes 1966112 | tf_op jit(solution)/shard_map/ppermute | solution.py:31
  83.5 3.0 %broadcast_select_fusion.refs_4_ = bf16[8,960,128]{2,1,0:T(8,128)(2,1)} fusion(bf16[8,960,128]{2,1,0:T(8,128)(2,1)S(1)} %copy-done.1, bf16[8,960,128]{2,1,0:T(8,128)(2,1)} %collective-permute-done.1, pred[]{:T(512)S(6)} %eq.7), kind=kLoop, calls=%fused_computation | loop fusion | flops 983040 | bytes 5898241 | tf_op jit(solution)/shard_map/jit(_where)/select_n | solution.py:604
  86.5 21.2 %apply_start.1 = (bf16[48,128,128]{2,1,0:T(8,128)(2,1)}, f32[8,128,128]{2,1,0:T(8,128)}) custom-call(s32[40]{0:T(128)} %get-tuple-element.28.slot_ref.refs_0_, s32[40]{0:T(128)} %get-tuple-element.29.local_ref.refs_1_, bf16[128,128]{1,0:T(8,128)(2,1)} %pad.4.mix_ref.refs_2_, bf16[8,960,128]{2,1,0:T(8,128)(2,1)} %fold_environment.2.refs_3_, ...), custom_call_target="tpu_custom_call" | custom-call | flops 10000000000 | bytes 10000000 | tf_op jit(solution)/shard_map/apply_start/pallas_call | solution.py:434
  107.7 26.7 %all_to_all.35 = bf16[16,3,128,128]{3,2,1,0:T(8,128)(2,1)} all-to-all(bf16[16,3,128,128]{3,2,1,0:T(8,128)(2,1)} %bitcast.23), channel_id=1, replica_groups=mesh['seg'=8,'sec'=16] {'sec'}, dimensions={0} | all-to-all | bytes 3145728 | tf_op jit(solution)/shard_map/all_to_all | solution.py:568
  134.5 6.9 %collect.3 = (f32[8,128,128]{2,1,0:T(8,128)}, f32[16,8,128]{2,1,0:T(8,128)}) custom-call(s32[40]{0:T(128)} %get-tuple-element.27.refs_0_, s32[8]{0:T(128)} %dynamic_slice.6.left_ref.refs_1_, s32[32]{0:T(128)} %reshape.32.right_ref.refs_2_, bf16[48,128,128]{2,1,0:T(8,128)(2,1)} %bitcast.17, f32[8,128,128]{2,1,0:T(8,128)} %get-tuple-element.33.refs_4_, ...), custom_call_target="tpu_custom_call" | custom-call | flops 10000000 | bytes 4000000 | tf_op jit(solution)/shard_map/collect/pallas_call | solution.py:512
  141.4 11.8 %all_to_all.36.refs_5_ = f32[16,8,128]{2,1,0:T(8,128)} all-to-all(f32[16,8,128]{2,1,0:T(8,128)} %get-tuple-element.35), channel_id=1, replica_groups=mesh['seg'=8,'sec'=16] {'sec'}, dimensions={0} | all-to-all | bytes 131072 | tf_op jit(solution)/shard_map/all_to_all | solution.py:568
  153.1 21.8 %apply_first.1 = (f32[8,128,128]{2,1,0:T(8,128)}, f32[8,128,128]{2,1,0:T(8,128)}, f32[8,128,128]{2,1,0:T(8,128)}, bf16[48,128,128]{2,1,0:T(8,128)(2,1)}, f32[8,128,128]{2,1,0:T(8,128)}) custom-call(s32[40]{0:T(128)} %get-tuple-element.28.slot_ref.refs_0_, s32[40]{0:T(128)} %get-tuple-element.29.local_ref.refs_1_, bf16[128,128]{1,0:T(8,128)(2,1)} %pad.4.mix_ref.refs_2_, ...), custom_call_target="tpu_custom_call" | custom-call | flops 10000000000 | bytes 10000000 | tf_op jit(solution)/shard_map/apply_first/pallas_call | solution.py:434
  174.9 24.9 %all_to_all.37 = bf16[16,3,128,128]{3,2,1,0:T(8,128)(2,1)} all-to-all(bf16[16,3,128,128]{3,2,1,0:T(8,128)(2,1)} %bitcast.22), channel_id=1, replica_groups=mesh['seg'=8,'sec'=16] {'sec'}, dimensions={0} | all-to-all | bytes 3145728 | tf_op jit(solution)/shard_map/all_to_all | solution.py:568
  199.8 7.5 %collect.4 = (f32[8,128,128]{2,1,0:T(8,128)}, f32[16,8,128]{2,1,0:T(8,128)}) custom-call(s32[40]{0:T(128)} %get-tuple-element.27.refs_0_, s32[8]{0:T(128)} %dynamic_slice.6.left_ref.refs_1_, s32[32]{0:T(128)} %reshape.32.right_ref.refs_2_, bf16[48,128,128]{2,1,0:T(8,128)(2,1)} %bitcast.18, f32[8,128,128]{2,1,0:T(8,128)} %get-tuple-element.38.refs_4_, ...), custom_call_target="tpu_custom_call" | custom-call | flops 10000000 | bytes 4000000 | tf_op jit(solution)/shard_map/collect/pallas_call | solution.py:512
  207.3 11.8 %all_to_all.38.refs_5_ = f32[16,8,128]{2,1,0:T(8,128)} all-to-all(f32[16,8,128]{2,1,0:T(8,128)} %get-tuple-element.42), channel_id=1, replica_groups=mesh['seg'=8,'sec'=16] {'sec'}, dimensions={0} | all-to-all | bytes 131072 | tf_op jit(solution)/shard_map/all_to_all | solution.py:568
  219.1 22.0 %apply_later.1 = (f32[8,128,128]{2,1,0:T(8,128)}, f32[8,128,128]{2,1,0:T(8,128)}, f32[8,128,128]{2,1,0:T(8,128)}, bf16[48,128,128]{2,1,0:T(8,128)(2,1)}, f32[8,128,128]{2,1,0:T(8,128)}) custom-call(s32[40]{0:T(128)} %get-tuple-element.28.slot_ref.refs_0_, s32[40]{0:T(128)} %get-tuple-element.29.local_ref.refs_1_, bf16[128,128]{1,0:T(8,128)(2,1)} %pad.4.mix_ref.refs_2_, ...), custom_call_target="tpu_custom_call" | custom-call | flops 10000000000 | bytes 10000000 | tf_op jit(solution)/shard_map/apply_later/pallas_call | solution.py:434
  241.1 22.8 %all_to_all.39 = bf16[16,3,128,128]{3,2,1,0:T(8,128)(2,1)} all-to-all(bf16[16,3,128,128]{3,2,1,0:T(8,128)(2,1)} %bitcast.21), channel_id=1, replica_groups=mesh['seg'=8,'sec'=16] {'sec'}, dimensions={0} | all-to-all | bytes 3145728 | tf_op jit(solution)/shard_map/all_to_all | solution.py:568
  263.8 7.0 %collect.5 = (f32[8,128,128]{2,1,0:T(8,128)}, f32[16,8,128]{2,1,0:T(8,128)}) custom-call(s32[40]{0:T(128)} %get-tuple-element.27.refs_0_, s32[8]{0:T(128)} %dynamic_slice.6.left_ref.refs_1_, s32[32]{0:T(128)} %reshape.32.right_ref.refs_2_, bf16[48,128,128]{2,1,0:T(8,128)(2,1)} %bitcast.16, f32[8,128,128]{2,1,0:T(8,128)} %get-tuple-element.45.refs_4_, ...), custom_call_target="tpu_custom_call" | custom-call | flops 10000000 | bytes 4000000 | tf_op jit(solution)/shard_map/collect/pallas_call | solution.py:512
  270.8 11.8 %all_to_all.40.gram_ref = f32[16,8,128]{2,1,0:T(8,128)} all-to-all(f32[16,8,128]{2,1,0:T(8,128)} %get-tuple-element.49), channel_id=1, replica_groups=mesh['seg'=8,'sec'=16] {'sec'}, dimensions={0} | all-to-all | bytes 131072 | tf_op jit(solution)/shard_map/all_to_all | solution.py:568
  282.6 5.7 %finish.1 = (f32[8,64,256]{2,1,0:T(8,128)}, f32[8,128]{1,0:T(8,128)}) custom-call(f32[16,8,128]{2,1,0:T(8,128)} %all_to_all.40.gram_ref, f32[8,128,128]{2,1,0:T(8,128)} %get-tuple-element.48.refs_7_.x_ref, f32[8,128,128]{2,1,0:T(8,128)} %get-tuple-element.47.refs_6_.d_ref), custom_call_target="tpu_custom_call" | custom-call | flops 1000000 | bytes 2000000 | tf_op jit(solution)/shard_map/finish/pallas_call | solution.py:549
  (24 shorter events, 7.8 us)
Async XLA Ops:
  0.6 59.1 %copy-start = (s32[128,4]{0,1:T(4,128)S(1)}, s32[128,4]{0,1:T(4,128)}, u32[]{:S(2)}) copy-start(s32[128,4]{0,1:T(4,128)} %param.19) | copy-start | bytes 6148
  0.6 17.5 %copy-start.2 = (bf16[1,8,64,1920]{3,2,1,0:T(8,128)(2,1)S(1)}, bf16[1,8,64,1920]{3,2,1,0:T(8,128)(2,1)}, u32[]{:S(2)}) copy-start(bf16[1,8,64,1920]{3,2,1,0:T(8,128)(2,1)} %param.11) | copy-start | bytes 5898244
  0.7 19.4 %copy-start.4 = (s32[30,30]{1,0:T(8,128)S(1)}, s32[30,30]{1,0:T(8,128)}, u32[]{:S(2)}) copy-start(s32[30,30]{1,0:T(8,128)} %param.16) | copy-start | bytes 10804
  0.7 19.4 %copy-start.3 = (bf16[30,4,30,4]{2,3,1,0:T(4,128)(2,1)S(1)}, bf16[30,4,30,4]{2,3,1,0:T(4,128)(2,1)}, u32[]{:S(2)}) copy-start(bf16[30,4,30,4]{2,3,1,0:T(4,128)(2,1)} %param.15) | copy-start | bytes 86404
  10.0 32.7 %all-to-all-start = ((bf16[16,3,64,256]{3,2,1,0:T(8,128)(2,1)}), bf16[16,3,64,256]{3,2,1,0:T(8,128)(2,1)}, u32[]{:S(2)}, u32[]{:S(2)}) async-start(bf16[16,3,64,256]{3,2,1,0:T(8,128)(2,1)} %get-tuple-element.30), calls=%async_computation | async-start | bytes 3145728 | tf_op jit(solution)/shard_map/all_to_all | solution.py:568
  18.1 48.6 %collective-permute-start = (bf16[8,64,1920]{2,1,0:T(8,128)(2,1)S(1)}, bf16[8,64,1920]{2,1,0:T(8,128)(2,1)}, u32[]{:S(2)}, u32[]{:S(2)}) collective-permute-start(bf16[8,64,1920]{2,1,0:T(8,128)(2,1)S(1)} %bitcast.20), channel_id=1, source_target_pairs={{16,0},{32,16},{48,32},{64,48},{80,64},{96,80},{112,96},{17,1},{33... | collective-permute-start | bytes 5898248 | tf_op jit(solution)/shard_map/ppermute | solution.py:31
  42.7 16.4 %copy-start.5 = (s32[128]{0:T(128)S(1)}, s32[128]{0:T(128)}, u32[]{:S(2)}) copy-start(s32[128]{0:T(128)} %param.18) | copy-start | bytes 1540
  57.2 26.3 %collective-permute-start.1 = (bf16[8,960,128]{2,1,0:T(8,128)(2,1)}, bf16[8,960,128]{2,1,0:T(8,128)(2,1)}, u32[]{:S(2)}, u32[]{:S(2)}) collective-permute-start(bf16[8,960,128]{2,1,0:T(8,128)(2,1)} %build_environment.1), channel_id=1, source_target_pairs={{0,16},{16,32},{32,48},{48,64},{64,80},{80,96},{96,112},{1,17},{17... | collective-permute-start | bytes 5898248 | tf_op jit(solution)/shard_map/ppermute | solution.py:31
  70.0 13.4 %copy-start.1 = (bf16[8,960,128]{2,1,0:T(8,128)(2,1)S(1)}, bf16[8,960,128]{2,1,0:T(8,128)(2,1)}, u32[]{:S(2)}) copy-start(bf16[8,960,128]{2,1,0:T(8,128)(2,1)} %fold_environment.3.env_ref) | copy-start | bytes 5898244

commit v3 on v2

--- a/solution.py
+++ b/solution.py
@@ -90,9 +90,8 @@
             owner = target // SEC_DEV
             rank = count[owner]
             count[owner] = rank + 1
-            slot = owner * slots + jnp.minimum(rank, slots - 1)
-            slot_ref[l * CLASSES + k] = jnp.where(owner == me, -1, slot)
-            local_ref[l * CLASSES + k] = target % SEC_DEV
+            slot_ref[l * CLASSES + k] = owner * slots + jnp.minimum(rank, slots - 1)
+            local_ref[l * CLASSES + k] = jnp.where(owner == me, target % SEC_DEV, -1)
 
     def one_group(g, carry):
         rank = jnp.int32(0)
@@ -139,24 +138,33 @@
     )(me, sector_shift, site)
 
 
-def fold_environment_kernel(in_ref, out_ref):
-    for i in range(W // 2):
-        pair = in_ref[0, :, i * FOLD : (i + 1) * FOLD].astype(F32)
-        first, second = fold_pair(pair)
-        out_ref[0, (2 * i) * HALF : (2 * i + 1) * HALF, :] = first.astype(BF)
-        out_ref[0, (2 * i + 1) * HALF : (2 * i + 2) * HALF, :] = second.astype(BF)
-
-
-def fold_environment(environment):
+def fold_environment_kernel(flag_ref, *refs):
+    out_ref = refs[-1]
+    for n in range(out_ref.shape[0]):
+        for i in range(W // 2):
+            pairs = [ref[n, :, i * FOLD : (i + 1) * FOLD].astype(F32) for ref in refs[:-1]]
+            pair = pairs[0] if len(pairs) == 1 else jnp.where(flag_ref[0] == 1, pairs[0], pairs[1])
+            first, second = fold_pair(pair)
+            out_ref[n, (2 * i) * HALF : (2 * i + 1) * HALF, :] = first.astype(BF)
+            out_ref[n, (2 * i + 1) * HALF : (2 * i + 2) * HALF, :] = second.astype(BF)
+
+
+def fold_environment(flag, *environments):
+    step = 2
     return pl.pallas_call(
         fold_environment_kernel,
-        grid=(SEC_DEV,),
         out_shape=jax.ShapeDtypeStruct((SEC_DEV, ROWS, FOLD), BF),
-        in_specs=[pl.BlockSpec((1, B, W * B), lambda l: (l, 0, 0))],
-        out_specs=pl.BlockSpec((1, ROWS, FOLD), lambda l: (l, 0, 0)),
+        grid_spec=pltpu.PrefetchScalarGridSpec(
+            num_scalar_prefetch=1,
+            grid=(SEC_DEV // step,),
+            in_specs=[pl.BlockSpec((step, B, W * B), lambda l, *refs: (l, 0, 0))] * len(environments),
+            out_specs=pl.BlockSpec((step, ROWS, FOLD), lambda l, *refs: (l, 0, 0)),
+        ),
         name="fold_environment",
-        cost_estimate=pl.CostEstimate(flops=0, bytes_accessed=4 * SEC_DEV * ROWS * FOLD, transcendentals=0),
-    )(environment)
+        cost_estimate=pl.CostEstimate(
+            flops=0, bytes_accessed=4 * SEC_DEV * ROWS * FOLD, transcendentals=0
+        ),
+    )(flag, *environments)
 
 
 def live_mask(left_size, right_sizes):
@@ -170,26 +178,28 @@
 
 
 def fold_state_kernel(left_ref, right_ref, state_ref, weight_ref, start_ref, fold_ref):
-    l = pl.program_id(0)
-    mask = live_mask(left_ref[l], [right_ref[l * D + t] for t in range(D)])
-    for source, result in ((state_ref, start_ref), (weight_ref, fold_ref)):
-        tiles = []
-        for i in range(D // 2):
-            tiles.extend(fold_pair(source[0, :, i * FOLD : (i + 1) * FOLD]))
-        folded = jnp.concatenate(tiles, axis=0)
-        result[0] = mask * folded if result is start_ref else folded
+    for n in range(state_ref.shape[0]):
+        l = pl.program_id(0) * state_ref.shape[0] + n
+        mask = live_mask(left_ref[l], [right_ref[l * D + t] for t in range(D)])
+        for source, result in ((state_ref, start_ref), (weight_ref, fold_ref)):
+            tiles = []
+            for i in range(D // 2):
+                tiles.extend(fold_pair(source[n, :, i * FOLD : (i + 1) * FOLD]))
+            folded = jnp.concatenate(tiles, axis=0)
+            result[n] = mask * folded if result is start_ref else folded
 
 
 def fold_state(left_sizes, right_sizes, state, weight):
-    natural = pl.BlockSpec((1, B, D * B), lambda l, *refs: (l, 0, 0))
-    folded = pl.BlockSpec((1, TILE, FOLD), lambda l, *refs: (l, 0, 0))
+    step = 4
+    natural = pl.BlockSpec((step, B, D * B), lambda l, *refs: (l, 0, 0))
+    folded = pl.BlockSpec((step, TILE, FOLD), lambda l, *refs: (l, 0, 0))
     shape = jax.ShapeDtypeStruct((SEC_DEV, TILE, FOLD), F32)
     return pl.pallas_call(
         fold_state_kernel,
         out_shape=(shape, shape),
         grid_spec=pltpu.PrefetchScalarGridSpec(
             num_scalar_prefetch=2,
-            grid=(SEC_DEV,),
+            grid=(SEC_DEV // step,),
             in_specs=[natural, natural],
             out_specs=(folded, folded),
         ),
@@ -212,64 +222,74 @@
     )
 
 
-def build_kernel(slot_ref, local_ref, env_ref, own_ref, came_ref, mix_ref, out_ref, first, second):
-    l = pl.program_id(0)
-
-    @pl.when(l == 0)
+def build_kernel(half, slot_ref, local_ref, env_ref, own_ref, came_ref, mix_ref, out_ref, *scratch):
+    size = env_ref.shape[0]
+    base = half + pl.program_id(0) * size
+
+    @pl.when(pl.program_id(0) == 0)
     def _():
-        first[W * D * PITCH :, :] = jnp.zeros(((MIX - W * D) * PITCH, FOLD), F32)
+        for first in scratch[:size]:
+            first[W * D * PITCH :, :] = jnp.zeros(((MIX - W * D) * PITCH, FOLD), F32)
 
     mix_turned = mix_ref[...].astype(F32).T.astype(BF)
-    for k in range(CLASSES):
-        slot = slot_ref[l * CLASSES + k]
-        local = local_ref[l * CLASSES + k]
-        tensor = jnp.where(slot < 0, own_ref[local], came_ref[jnp.maximum(slot, 0)])
-        blocks = []
+    for n in range(size):
+        first = scratch[n]
+        for k in range(CLASSES):
+            slot = slot_ref[(base + n) * CLASSES + k]
+            local = local_ref[(base + n) * CLASSES + k]
+            tensor = jnp.where(local >= 0, own_ref[jnp.maximum(local, 0)], came_ref[slot])
+            blocks = []
+            for i in range(D // 2):
+                blocks.extend(spread_pair(tensor[:, i * FOLD : (i + 1) * FOLD].astype(F32)))
+            right = jnp.concatenate(blocks, axis=1).astype(BF)
+            left = env_ref[n, k * GROUP * HALF : (k + 1) * GROUP * HALF, :]
+            joined = dot(left, right)
+            for j in range(GROUP):
+                for t in range(D):
+                    at = ((k * GROUP + j) * D + t) * PITCH
+                    first[at : at + HALF, :] = joined[j * HALF : (j + 1) * HALF, t * FOLD : (t + 1) * FOLD]
+    for n in range(size):
+        mix_channels(mix_turned, scratch[n], scratch[size + n])
+    low_half = low_lanes(HALF)
+    low = low_lanes(B)
+    for n in range(size):
+        second = scratch[size + n]
+        own = own_ref[base + n]
+        tiles = []
         for i in range(D // 2):
-            blocks.extend(spread_pair(tensor[:, i * FOLD : (i + 1) * FOLD].astype(F32)))
-        right = jnp.concatenate(blocks, axis=1).astype(BF)
-        left = env_ref[0, k * GROUP * HALF : (k + 1) * GROUP * HALF, :]
-        joined = dot(left, right)
-        for j in range(GROUP):
-            for t in range(D):
-                at = ((k * GROUP + j) * D + t) * PITCH
-                first[at : at + HALF, :] = joined[j * HALF : (j + 1) * HALF, t * FOLD : (t + 1) * FOLD]
-    mix_channels(mix_turned, first, second)
-    own = own_ref[l]
-    tiles = []
-    low_half = low_lanes(HALF)
-    for i in range(D // 2):
-        pair = own[:, i * FOLD : (i + 1) * FOLD].astype(F32)
-        rolled = pltpu.roll(pair, B, 1)
-        tiles.append(jnp.where(low_half, pair[:HALF], rolled[HALF:]))
-        tiles.append(jnp.where(low_half, rolled[:HALF], pair[HALF:]))
-    turned = jnp.concatenate(tiles, axis=0).T.astype(BF)
-    low = low_lanes(B)
-    for v in range(0, W, 2):
-        right = jnp.concatenate(
-            [mixed_rows(second, v + i) for i in range(2)], axis=1
-        )
-        product = dot(turned, right)
-        for i in range(2):
-            block = product[:, i * FOLD : (i + 1) * FOLD]
-            chosen = jnp.where(low, block[:B], block[B:])
-            total = chosen + pltpu.roll(chosen, B, 1)
-            folded = jnp.where(low_half, total[:HALF], total[HALF:])
-            out_ref[0, (v + i) * HALF : (v + i + 1) * HALF, :] = folded.astype(BF)
-
-
-def build_environment(slot, local, environment, site, came, mix):
-    folded = pl.BlockSpec((1, ROWS, FOLD), lambda l, *refs: (l, 0, 0))
+            pair = own[:, i * FOLD : (i + 1) * FOLD].astype(F32)
+            rolled = pltpu.roll(pair, B, 1)
+            tiles.append(jnp.where(low_half, pair[:HALF], rolled[HALF:]))
+            tiles.append(jnp.where(low_half, rolled[:HALF], pair[HALF:]))
+        turned = jnp.concatenate(tiles, axis=0).T.astype(BF)
+        for v in range(0, W, 2):
+            right = jnp.concatenate([mixed_rows(second, v + i) for i in range(2)], axis=1)
+            product = dot(turned, right)
+            for i in range(2):
+                block = product[:, i * FOLD : (i + 1) * FOLD]
+                chosen = jnp.where(low, block[:B], block[B:])
+                total = chosen + pltpu.roll(chosen, B, 1)
+                folded = jnp.where(low_half, total[:HALF], total[HALF:])
+                out_ref[n, (v + i) * HALF : (v + i + 1) * HALF, :] = folded.astype(BF)
+
+
+def build_environment(half, sectors, slot, local, environment, site, came, mix):
+    step = 2
     whole = lambda shape: pl.BlockSpec(shape, lambda l, *refs: (0,) * len(shape))
     return pl.pallas_call(
-        build_kernel,
-        out_shape=jax.ShapeDtypeStruct((SEC_DEV, ROWS, FOLD), BF),
+        functools.partial(build_kernel, half),
+        out_shape=jax.ShapeDtypeStruct((sectors, ROWS, FOLD), BF),
         grid_spec=pltpu.PrefetchScalarGridSpec(
             num_scalar_prefetch=2,
-            grid=(SEC_DEV,),
-            in_specs=[folded, whole(site.shape), whole(came.shape), whole(mix.shape)],
-            out_specs=folded,
-            scratch_shapes=[pltpu.VMEM((MIX * PITCH, FOLD), F32), pltpu.VMEM((MIX * PITCH, FOLD), F32)],
+            grid=(sectors // step,),
+            in_specs=[
+                pl.BlockSpec((step, ROWS, FOLD), lambda l, *refs: (l + half // step, 0, 0)),
+                whole(site.shape),
+                whole(came.shape),
+                whole(mix.shape),
+            ],
+            out_specs=pl.BlockSpec((step, ROWS, FOLD), lambda l, *refs: (l, 0, 0)),
+            scratch_shapes=[pltpu.VMEM((MIX * PITCH, FOLD), F32)] * (2 * step),
         ),
         name="build_environment",
         cost_estimate=pl.CostEstimate(flops=10**10, bytes_accessed=10**7, transcendentals=0),
@@ -357,99 +377,115 @@
 
 
 def apply_kernel(mode, entries, *refs):
-    slot_ref, local_ref, mix_ref, right_ref, left_ref = refs[:5]
-    refs = refs[5:]
-    l = pl.program_id(0)
+    flag_ref, slot_ref, local_ref, mix_ref, right_ref, left_ref, early_ref, late_ref = refs[:8]
+    refs = refs[8:]
+    step_at = pl.program_id(0)
     if mode == "start":
-        state_ref, send_ref, own_ref, first, second, fixed = refs
+        state_ref, send_ref, own_ref = refs[:3]
+        scratch = refs[3:]
     elif mode == "first":
         gram_ref, u_ref, h_ref, weight_ref = refs[:4]
-        x_out, a_out, d_out, send_ref, own_ref, first, second, fixed = refs[4:]
+        x_out, a_out, d_out, send_ref, own_ref = refs[4:9]
+        scratch = refs[9:]
     else:
         gram_ref, x_ref, a_ref, d_ref, p_ref, weight_ref = refs[:6]
-        x_out, a_out, d_out, send_ref, own_ref, first, second, fixed = refs[6:]
-
-    @pl.when(l == 0)
+        x_out, a_out, d_out, send_ref, own_ref = refs[6:11]
+        scratch = refs[11:]
+    fixed, partials = scratch[:2]
+    scratch = scratch[2:]
+    size = right_ref.shape[0]
+
+    @pl.when(step_at == 0)
     def _():
         own_ref[...] = jnp.zeros_like(own_ref)
-        first[W * D * PITCH :, :] = jnp.zeros(((MIX - W * D) * PITCH, FOLD), F32)
+        for first in scratch[:size]:
+            first[W * D * PITCH :, :] = jnp.zeros(((MIX - W * D) * PITCH, FOLD), F32)
         if mode != "start":
             scalars = first_scalars if mode == "first" else later_scalars
             for i, value in enumerate(scalars(gram_ref, entries)):
                 fixed[i : i + 1, :] = jnp.broadcast_to(value, (1, FOLD))
 
-    if mode == "start":
-        vector = state_ref[0]
-    else:
-        if mode == "first":
-            inverse, rho, along, norm = [fixed[i : i + 1, :] for i in range(4)]
-            current = inverse * u_ref[0]
-            applied = inverse * h_ref[0]
+    for n in range(size):
+        first = scratch[n]
+        if mode == "start":
+            vector = state_ref[n]
         else:
-            cosine, sine, rho, along, norm = [fixed[i : i + 1, :] for i in range(5)]
-            current = cosine * x_ref[0] + sine * d_ref[0]
-            applied = cosine * a_ref[0] + sine * p_ref[0]
-        vector = (weight_ref[0] * (applied - rho * current) - along * current) * norm
-        x_out[0] = current
-        a_out[0] = applied
-        d_out[0] = vector
-
-    right = jnp.concatenate(
-        [spread(vector[s * HALF : (s + 1) * HALF]) for s in range(D)], axis=1
-    ).astype(BF)
-    step = GROUP * HALF
-    for i in range(CLASSES):
-        product = dot(right_ref[0, i * step : (i + 1) * step, :], right)
-        for v in range(GROUP):
-            for s in range(D):
-                at = ((i * GROUP + v) * D + s) * PITCH
-                first[at : at + HALF, :] = product[v * HALF : (v + 1) * HALF, s * FOLD : (s + 1) * FOLD]
-    mix_channels(mix_ref[...], first, second)
-    for k in range(CLASSES):
-        rows, blocks = [], []
-        for w in range(k * GROUP, (k + 1) * GROUP):
-            rows.append(mixed_rows(second, w))
-            blocks.append(spread(left_ref[0, w * HALF : (w + 1) * HALF, :].astype(F32)).astype(BF))
-        partial = dot(jnp.concatenate(rows, axis=1), jnp.concatenate(blocks, axis=0))
-        slot = slot_ref[l * CLASSES + k]
-        local = local_ref[l * CLASSES + k]
-
-        @pl.when(slot >= 0)
-        def _():
-            send_ref[jnp.maximum(slot, 0)] = partial.astype(BF)
-
-        @pl.when(slot < 0)
-        def _():
-            own_ref[local] = own_ref[local] + partial
-
-
-def apply_operator(mode, entries, slots_total, slot, local, mix, right_env, left_env, gram, vectors):
-    vector = pl.BlockSpec((1, TILE, FOLD), lambda l, *refs: (l, 0, 0))
-    folded = pl.BlockSpec((1, ROWS, FOLD), lambda l, *refs: (l, 0, 0))
+            if mode == "first":
+                inverse, rho, along, norm = [fixed[i : i + 1, :] for i in range(4)]
+                current = inverse * u_ref[n]
+                applied = inverse * h_ref[n]
+            else:
+                cosine, sine, rho, along, norm = [fixed[i : i + 1, :] for i in range(5)]
+                current = cosine * x_ref[n] + sine * d_ref[n]
+                applied = cosine * a_ref[n] + sine * p_ref[n]
+            vector = (weight_ref[n] * (applied - rho * current) - along * current) * norm
+            x_out[n] = current
+            a_out[n] = applied
+            d_out[n] = vector
+        right = jnp.concatenate(
+            [spread(vector[s * HALF : (s + 1) * HALF]) for s in range(D)], axis=1
+        ).astype(BF)
+        rows = GROUP * HALF
+        for i in range(CLASSES):
+            product = dot(right_ref[n, i * rows : (i + 1) * rows, :], right)
+            for v in range(GROUP):
+                for s in range(D):
+                    at = ((i * GROUP + v) * D + s) * PITCH
+                    first[at : at + HALF, :] = product[v * HALF : (v + 1) * HALF, s * FOLD : (s + 1) * FOLD]
+    for n in range(size):
+        mix_channels(mix_ref[...], scratch[n], scratch[size + n])
+    own_left = flag_ref[0] == 1
+    early = step_at < SEC_DEV // 2 // size
+    for n in range(size):
+        for k in range(CLASSES):
+            rows, blocks = [], []
+            for w in range(k * GROUP, (k + 1) * GROUP):
+                at = slice(w * HALF, (w + 1) * HALF)
+                handed = jnp.where(early, early_ref[n, at, :], late_ref[n, at, :])
+                chosen = jnp.where(own_left, left_ref[n, at, :], handed)
+                rows.append(mixed_rows(scratch[size + n], w))
+                blocks.append(spread(chosen.astype(F32)).astype(BF))
+            partial = dot(jnp.concatenate(rows, axis=1), jnp.concatenate(blocks, axis=0))
+            partials[n * CLASSES + k] = partial
+            send_ref[slot_ref[(step_at * size + n) * CLASSES + k]] = partial.astype(BF)
+    for n in range(size):
+        for k in range(CLASSES):
+            local = local_ref[(step_at * size + n) * CLASSES + k]
+
+            @pl.when(local >= 0)
+            def _():
+                place = jnp.maximum(local, 0)
+                own_ref[place] = own_ref[place] + partials[n * CLASSES + k]
+
+
+def apply_operator(mode, entries, slots_total, flag, slot, local, mix, right_env, left_envs, gram, vectors):
+    step = 2
+    halves = SEC_DEV // step // 2
+    vector = pl.BlockSpec((step, TILE, FOLD), lambda l, *refs: (l, 0, 0))
+    folded = pl.BlockSpec((step, ROWS, FOLD), lambda l, *refs: (l, 0, 0))
+    early = pl.BlockSpec((step, ROWS, FOLD), lambda l, *refs: (jnp.minimum(l, halves - 1), 0, 0))
+    late = pl.BlockSpec((step, ROWS, FOLD), lambda l, *refs: (jnp.maximum(l - halves, 0), 0, 0))
     whole = lambda shape: pl.BlockSpec(shape, lambda l, *refs: (0,) * len(shape))
     shape = jax.ShapeDtypeStruct((SEC_DEV, TILE, FOLD), F32)
     kept = 0 if mode == "start" else 3
     send = jax.ShapeDtypeStruct((slots_total, TILE, FOLD), BF)
-    inputs = (mix, right_env, left_env) + (() if gram is None else (gram,)) + tuple(vectors)
+    inputs = (mix, right_env) + tuple(left_envs) + (() if gram is None else (gram,)) + tuple(vectors)
     return pl.pallas_call(
         functools.partial(apply_kernel, mode, entries),
         out_shape=(shape,) * kept + (send, shape),
         grid_spec=pltpu.PrefetchScalarGridSpec(
-            num_scalar_prefetch=2,
-            grid=(SEC_DEV,),
-            in_specs=[whole(mix.shape), folded, folded]
+            num_scalar_prefetch=3,
+            grid=(SEC_DEV // step,),
+            in_specs=[whole(mix.shape), folded, folded, early, late]
             + ([] if gram is None else [whole(gram.shape)])
             + [vector] * len(vectors),
             out_specs=(vector,) * kept + (whole(send.shape), whole(shape.shape)),
-            scratch_shapes=[
-                pltpu.VMEM((MIX * PITCH, FOLD), F32),
-                pltpu.VMEM((MIX * PITCH, FOLD), F32),
-                pltpu.VMEM((8, FOLD), F32),
-            ],
+            scratch_shapes=[pltpu.VMEM((8, FOLD), F32), pltpu.VMEM((step * CLASSES, TILE, FOLD), F32)]
+            + [pltpu.VMEM((MIX * PITCH, FOLD), F32)] * (2 * step),
         ),
         name="apply_" + mode,
         cost_estimate=pl.CostEstimate(flops=10**10, bytes_accessed=10**7, transcendentals=0),
-    )(slot, local, *inputs)
+    )(flag, slot, local, *inputs)
 
 
 def collect_kernel(names, *refs):
@@ -465,47 +501,51 @@
         at += 1
     out_ref, gram_ref, sums = refs[at:]
     result = "h" if names is FIRST else "p"
-    m = pl.program_id(0)
-
-    @pl.when(m == 0)
+    step_at = pl.program_id(0)
+    count = own_ref.shape[0]
+
+    @pl.when(step_at == 0)
     def _():
         sums[...] = jnp.zeros_like(sums)
 
-    total = own_ref[0]
-    for k in range(CLASSES):
-        place = take_ref[k * SEC_DEV + m]
-        part = came_ref[jnp.maximum(place, 0)].astype(F32)
-        total = total + jnp.where(place >= 0, part, 0.0)
-    total = live_mask(left_ref[m], [right_ref[m * D + t] for t in range(D)]) * total
-    out_ref[0] = total
     size = 8
-    totals = [jnp.zeros((size, FOLD), F32) for name in names]
-    for i in range(TILE // size):
-        rows = slice(i * size, (i + 1) * size)
-        value = {symbol: ref[0, rows, :] for symbol, ref in zip(symbols, vectors)}
-        value[result] = total[rows]
-        if weighted:
-            weight = weight_ref[0, rows, :]
-            for symbol in list(value):
-                value["P" + symbol] = weight * value[symbol]
-        for n, name in enumerate(names):
-            one, two = split_name(name)
-            totals[n] = totals[n] + value[one] * value[two]
-    for n in range(len(names)):
-        sums[n] = sums[n] + totals[n]
-
-    @pl.when(m == SEC_DEV - 1)
+    for n in range(count):
+        m = step_at * count + n
+        total = own_ref[n]
+        for k in range(CLASSES):
+            place = take_ref[k * SEC_DEV + m]
+            part = came_ref[jnp.maximum(place, 0)].astype(F32)
+            total = total + jnp.where(place >= 0, part, 0.0)
+        total = live_mask(left_ref[m], [right_ref[m * D + t] for t in range(D)]) * total
+        out_ref[n] = total
+        totals = [jnp.zeros((size, FOLD), F32) for name in names]
+        for i in range(TILE // size):
+            rows = slice(i * size, (i + 1) * size)
+            value = {symbol: ref[n, rows, :] for symbol, ref in zip(symbols, vectors)}
+            value[result] = total[rows]
+            if weighted:
+                weight = weight_ref[n, rows, :]
+                for symbol in list(value):
+                    value["P" + symbol] = weight * value[symbol]
+            for at, name in enumerate(names):
+                one, two = split_name(name)
+                totals[at] = totals[at] + value[one] * value[two]
+        for at in range(len(names)):
+            sums[at] = sums[at] + totals[at]
+
+    @pl.when(step_at == SEC_DEV // count - 1)
     def _():
         lane = lax.broadcasted_iota(jnp.int32, (8, FOLD), 1)
         packed = jnp.zeros((8, FOLD), F32)
-        for n in range(len(names)):
-            packed = jnp.where(lane == n, jnp.sum(sums[n], keepdims=True), packed)
+        for at in range(len(names)):
+            packed = jnp.where(lane == at, jnp.sum(sums[at], keepdims=True), packed)
         for g in range(gram_ref.shape[0]):
             gram_ref[g] = packed
 
 
 def collect(names, groups, take, left_sizes, right_sizes, came, own, vectors, weight):
-    vector = pl.BlockSpec((1, TILE, FOLD), lambda m, *refs: (m, 0, 0))
+    step = 4
+    vector = pl.BlockSpec((step, TILE, FOLD), lambda m, *refs: (m, 0, 0))
     whole = lambda shape: pl.BlockSpec(shape, lambda m, *refs: (0,) * len(shape))
     extra = () if weight is None else (weight,)
     gram = jax.ShapeDtypeStruct((groups, 8, FOLD), F32)
@@ -514,7 +554,7 @@
         out_shape=(jax.ShapeDtypeStruct((SEC_DEV, TILE, FOLD), F32), gram),
         grid_spec=pltpu.PrefetchScalarGridSpec(
             num_scalar_prefetch=3,
-            grid=(SEC_DEV,),
+            grid=(SEC_DEV // step,),
             in_specs=[whole(came.shape)] + [vector] * (1 + len(vectors) + len(extra)),
             out_specs=(vector, whole(gram.shape)),
             scratch_shapes=[pltpu.VMEM((len(names), 8, FOLD), F32)],
@@ -537,25 +577,27 @@
         fixed[1:2, :] = jnp.broadcast_to(sine, (1, FOLD))
         energy_ref[...] = jnp.broadcast_to(energy, energy_ref.shape)
 
-    final = fixed[0:1, :] * x_ref[0] + fixed[1:2, :] * d_ref[0]
-    for i in range(D // 2):
-        first = final[(2 * i) * HALF : (2 * i + 1) * HALF]
-        second = final[(2 * i + 1) * HALF : (2 * i + 2) * HALF]
-        state_ref[0, :, i * FOLD : (i + 1) * FOLD] = unfold_pair(first, second)
+    for n in range(x_ref.shape[0]):
+        final = fixed[0:1, :] * x_ref[n] + fixed[1:2, :] * d_ref[n]
+        for i in range(D // 2):
+            first = final[(2 * i) * HALF : (2 * i + 1) * HALF]
+            second = final[(2 * i + 1) * HALF : (2 * i + 2) * HALF]
+            state_ref[n, :, i * FOLD : (i + 1) * FOLD] = unfold_pair(first, second)
 
 
 def finish(entries, gram, current, direction):
-    vector = pl.BlockSpec((1, TILE, FOLD), lambda l: (l, 0, 0))
+    step = 4
+    vector = pl.BlockSpec((step, TILE, FOLD), lambda l: (l, 0, 0))
     return pl.pallas_call(
         functools.partial(finish_kernel, entries),
-        grid=(SEC_DEV,),
+        grid=(SEC_DEV // step,),
         out_shape=(
             jax.ShapeDtypeStruct((SEC_DEV, B, D * B), F32),
             jax.ShapeDtypeStruct((8, FOLD), F32),
         ),
         in_specs=[pl.BlockSpec(gram.shape, lambda l: (0, 0, 0)), vector, vector],
         out_specs=(
-            pl.BlockSpec((1, B, D * B), lambda l: (l, 0, 0)),
+            pl.BlockSpec((step, B, D * B), lambda l: (l, 0, 0)),
             pl.BlockSpec((8, FOLD), lambda l: (0, 0)),
         ),
         scratch_shapes=[pltpu.VMEM((8, FOLD), F32)],
@@ -590,24 +632,29 @@
     position = lax.axis_index("seg")
     last = lax.axis_size("seg") - 1
 
+    at_end = (position == last).astype(jnp.int32)[None]
+    at_start = (position == 0).astype(jnp.int32)[None]
     came_right = passed_along(right_environment[0], "seg", -1)
-    right_used = jnp.where(position == last, right_environment[0], came_right)
 
     slot, local, take, site_send = route(my_group[None], sector_shift, site_previous[0], groups, slots)
     site_came = exchange(site_send).reshape(groups * slots, B, D * B)
     mix = channel_tensor * channel_mask.astype(BF)[:, None, :, None]
     mix = jnp.pad(mix.reshape(W * D, W * D), ((0, MIX - W * D), (0, MIX - W * D)))
 
-    own_left = fold_environment(left_environment[0])
-    fresh = build_environment(slot, local, own_left, site_previous[0], site_came, mix)
-    handed = passed_along(fresh, "seg", 1)
-    left_env = jnp.where(position == 0, own_left, handed)
-    right_env = fold_environment(right_used)
+    own_left = fold_environment(at_start, left_environment[0])
+    handed = []
+    for half in range(2):
+        sectors = SEC_DEV // 2
+        fresh = build_environment(
+            half * sectors, sectors, slot, local, own_left, site_previous[0], site_came, mix
+        )
+        handed.append(passed_along(fresh, "seg", 1))
+    right_env = fold_environment(at_end, right_environment[0], came_right)
     start, weight = fold_state(my_left, my_right, state_start[0], preconditioner[0])
 
     apply = functools.partial(
-        apply_operator, entries=entries, slots_total=groups * slots, slot=slot, local=local, mix=mix,
-        right_env=right_env, left_env=left_env,
+        apply_operator, entries=entries, slots_total=groups * slots, flag=at_start, slot=slot, local=local,
+        mix=mix, right_env=right_env, left_envs=(own_left, *handed),
     )
 
     def gather(names, send, own, vectors, weight):

time: 292 us -> 246 us (0.84)
  Pallas kernels: 136 us -> 88.8 us
  other arithmetic: 6.4 us -> 0.07 us
  waiting for transfers between devices: 18.6 us -> 24.2 us
  starting transfers between devices: 11.9 us -> 15.6 us
    pallas_call x3, Pallas kernels: 65 us -> 35.8 us  [apply_operator(): pl.pallas_call(functools.partial(apply_kernel, mode, entries), out_shape=...]
    pallas_call x3, Pallas kernels: 21.4 us -> 12.7 us  [collect(): pl.pallas_call(functools.partial(collect_kernel, names), out_shape=(jax.S...]
    pallas_call x4 -> x5, Pallas kernels: 34.4 us -> 27.8 us  [the longest x2 14.2 us: build_environment(): pl.pallas_call(functools.partial(build_kernel, half), out_shape=jax.Shape...]
    select_n x2 -> x0, other arithmetic: 6.33 us -> none  [the longest x1 3.29 us: on_device(): right_used = jnp.where(position == last, right_environment[0], came_right)]
    ppermute x2 -> x3, waiting for transfers between devices: 6.29 us -> 10.3 us  [passed_along(): return lax.ppermute(block, axis, route)]
    ppermute x2 -> x3, starting transfers between devices: 3.83 us -> 7.33 us  [passed_along(): return lax.ppermute(block, axis, route)]
  transfers between devices with their start and end apart: 3 -> 4, of which waited for: 2 -> 2; matrix products, arithmetic and copies ran while one was open for 3% -> 2% of each run, Pallas kernels for 12% -> 12%
where the time goes in v3:
time: 246 us; the launch traced here: 245 us
  blocking collectives  110 us (45%)
  Pallas kernels  88.8 us (36%)
  waiting for transfers between devices  24.2 us (10%)
  starting transfers between devices  15.6 us (6%)
  local copies, waits for them, and re-layouts  5.82 us (2%)
    all_to_all x6, blocking collectives, exchange(): return lax.all_to_all(blocks, 'sec', 0, 0, tiled=True)  110 us
    pallas_call x3, Pallas kernels, apply_operator(): pl.pallas_call(functools.partial(apply_kernel, mode, entries), out_shape=...  35.8 us
    pallas_call x2, Pallas kernels, build_environment(): pl.pallas_call(functools.partial(build_kernel, half), out_shape=jax.Shape...  14.2 us
    all_to_all x1, waiting for transfers between devices, exchange(): return lax.all_to_all(blocks, 'sec', 0, 0, tiled=True)  13.9 us
    pallas_call x3, Pallas kernels, collect(): pl.pallas_call(functools.partial(collect_kernel, names), out_shape=(jax.S...  12.7 us
    pallas_call x2, Pallas kernels, fold_environment(): pl.pallas_call(fold_environment_kernel, out_shape=jax.ShapeDtypeStruct((S...  11.1 us
    ppermute x3, waiting for transfers between devices, passed_along(): return lax.ppermute(block, axis, route)  10.3 us
    pallas_call x1, Pallas kernels, route(): pl.pallas_call(route_kernel, out_shape=(jax.ShapeDtypeStruct((PAIRS,), jn...  9.13 us
  transfers between devices with their start and end apart: 4, of which 2 were waited for; matrix products, arithmetic and copies ran while one was open for 2% of the time, Pallas kernels for 12%

profile of v3, /device:TPU:2, one launch (start us, length us, event | category | flops | bytes accessed | tf_op | source)
XLA Modules:
  0.0 245.0 jit_solution(7990271771012772831)
XLA Ops:
  0.6 9.1 %route.1 = (s32[40]{0:T(128)}, s32[40]{0:T(128)}, s32[40]{0:T(128)}, bf16[16,3,64,256]{3,2,1,0:T(8,128)(2,1)}) custom-call(s32[1]{0:T(128)} %bitcast.me_ref, s32[5,128]{1,0:T(8,128)} %shift_ref.1, bf16[8,64,256]{2,1,0:T(8,128)(2,1)} %bitcast.28), custom_call_target="tpu_custom_call" | custom-call | tf_op jit(solution)/shard_map/route/pallas_call | solution.py:126
  9.8 8.2 %all-to-all-start = ((bf16[16,3,64,256]{3,2,1,0:T(8,128)(2,1)}), bf16[16,3,64,256]{3,2,1,0:T(8,128)(2,1)}, u32[]{:S(2)}, u32[]{:S(2)}) async-start(bf16[16,3,64,256]{3,2,1,0:T(8,128)(2,1)} %get-tuple-element.30), calls=%async_computation | async-start | bytes 3145728 | tf_op jit(solution)/shard_map/all_to_all | solution.py:610
  18.1 1.9 collective-permute-start
  23.4 5.4 %fold_environment.3.env_ref.refs_5_ = bf16[8,960,128]{2,1,0:T(8,128)(2,1)} custom-call(s32[1]{0:T(128)} %bitcast.2.flag_ref.refs_0_, bf16[8,64,1920]{2,1,0:T(8,128)(2,1)} %bitcast.20), custom_call_target="tpu_custom_call" | custom-call | bytes 3932160 | tf_op jit(solution)/shard_map/fold_environment/pallas_call | solution.py:154
  28.8 13.9 %all-to-all-done = bf16[16,3,64,256]{3,2,1,0:T(8,128)(2,1)} async-done(((bf16[16,3,64,256]{3,2,1,0:T(8,128)(2,1)}), bf16[16,3,64,256]{3,2,1,0:T(8,128)(2,1)}, u32[]{:S(2)}, u32[]{:S(2)}) %all-to-all-start) | async-done | bytes 1572896 | tf_op jit(solution)/shard_map/all_to_all | solution.py:610
  42.6 7.0 %build_environment.3 = bf16[4,960,128]{2,1,0:T(8,128)(2,1)} custom-call(s32[40]{0:T(128)} %get-tuple-element.28.slot_ref.refs_1_, s32[40]{0:T(128)} %get-tuple-element.29.local_ref.refs_2_, bf16[8,960,128]{2,1,0:T(8,128)(2,1)} %fold_environment.3.env_ref.refs_5_, bf16[8,64,256]{2,1,0:T(8,128)(2,1)} %bitcast.29, bf16[48,64,256]{2,1,0:T(8,128)(2,1)} %bitcast.6.came_ref, ...), custom_call_target="tpu_custom_call" | custom-call | flops 10000000000 | bytes 10000000 | tf_op jit(solution)/shard_map/build_environment/pallas_call | solution.py:279
  49.7 7.2 %build_environment.2 = bf16[4,960,128]{2,1,0:T(8,128)(2,1)} custom-call(s32[40]{0:T(128)} %get-tuple-element.28.slot_ref.refs_1_, s32[40]{0:T(128)} %get-tuple-element.29.local_ref.refs_2_, bf16[8,960,128]{2,1,0:T(8,128)(2,1)} %fold_environment.3.env_ref.refs_5_, bf16[8,64,256]{2,1,0:T(8,128)(2,1)} %bitcast.30, bf16[48,64,256]{2,1,0:T(8,128)(2,1)} %bitcast.6.came_ref, ...), custom_call_target="tpu_custom_call" | custom-call | flops 10000000000 | bytes 10000000 | tf_op jit(solution)/shard_map/build_environment/pallas_call | solution.py:279
  58.8 3.5 %collective-permute-start.2 = (bf16[4,960,128]{2,1,0:T(8,128)(2,1)}, bf16[4,960,128]{2,1,0:T(8,128)(2,1)}, u32[]{:S(2)}, u32[]{:S(2)}) collective-permute-start(bf16[4,960,128]{2,1,0:T(8,128)(2,1)} %build_environment.3), channel_id=1, source_target_pairs={{0,16},{16,32},{32,48},{48,64},{64,80},{80,96},{96,112},{1,17},{17... | collective-permute-start | bytes 2949128 | tf_op jit(solution)/shard_map/ppermute | solution.py:31
  63.6 3.5 %fold_state.1 = (f32[8,128,128]{2,1,0:T(8,128)}, f32[8,128,128]{2,1,0:T(8,128)}) custom-call(s32[8]{0:T(128)} %dynamic_slice.6.left_ref.refs_1_, s32[32]{0:T(128)} %reshape.32.right_ref.refs_2_, f32[8,64,256]{2,1,0:T(8,128)} %bitcast.26, f32[8,64,256]{2,1,0:T(8,128)} %bitcast.27), custom_call_target="tpu_custom_call" | custom-call | bytes 2097152 | tf_op jit(solution)/shard_map/fold_state/pallas_call | solution.py:197
  67.1 5.7 %fold_environment.2.refs_4_ = bf16[8,960,128]{2,1,0:T(8,128)(2,1)} custom-call(s32[1]{0:T(128)} %bitcast.3.flag_ref, bf16[8,64,1920]{2,1,0:T(8,128)(2,1)} %bitcast.21, bf16[8,64,1920]{2,1,0:T(8,128)(2,1)} %collective-permute-done.refs_1_), custom_call_target="tpu_custom_call" | custom-call | bytes 3932160 | tf_op jit(solution)/shard_map/fold_environment/pallas_call | solution.py:154
  72.8 10.3 %collective-permute-done.2.refs_7_ = bf16[4,960,128]{2,1,0:T(8,128)(2,1)} collective-permute-done((bf16[4,960,128]{2,1,0:T(8,128)(2,1)}, bf16[4,960,128]{2,1,0:T(8,128)(2,1)}, u32[]{:S(2)}, u32[]{:S(2)}) %collective-permute-start.2) | collective-permute-done | bytes 983072 | tf_op jit(solution)/shard_map/ppermute | solution.py:31
  83.1 11.6 %apply_start.1 = (bf16[48,128,128]{2,1,0:T(8,128)(2,1)}, f32[8,128,128]{2,1,0:T(8,128)}) custom-call(s32[1]{0:T(128)} %bitcast.2.flag_ref.refs_0_, s32[40]{0:T(128)} %get-tuple-element.28.slot_ref.refs_1_, s32[40]{0:T(128)} %get-tuple-element.29.local_ref.refs_2_, bf16[128,128]{1,0:T(8,128)(2,1)} %pad.4.mix_ref.refs_3_, ...), custom_call_target="tpu_custom_call" | custom-call | flops 10000000000 | bytes 10000000 | tf_op jit(solution)/shard_map/apply_start/pallas_call | solution.py:473
  94.7 26.7 %all_to_all.35 = bf16[16,3,128,128]{3,2,1,0:T(8,128)(2,1)} all-to-all(bf16[16,3,128,128]{3,2,1,0:T(8,128)(2,1)} %bitcast.25), channel_id=1, replica_groups=mesh['seg'=8,'sec'=16] {'sec'}, dimensions={0} | all-to-all | bytes 3145728 | tf_op jit(solution)/shard_map/all_to_all | solution.py:610
  121.4 4.0 %collect.3 = (f32[8,128,128]{2,1,0:T(8,128)}, f32[16,8,128]{2,1,0:T(8,128)}) custom-call(s32[40]{0:T(128)} %get-tuple-element.27.refs_0_, s32[8]{0:T(128)} %dynamic_slice.6.left_ref.refs_1_, s32[32]{0:T(128)} %reshape.32.right_ref.refs_2_, bf16[48,128,128]{2,1,0:T(8,128)(2,1)} %bitcast.18, f32[8,128,128]{2,1,0:T(8,128)} %get-tuple-element.33.refs_4_, ...), custom_call_target="tpu_custom_call" | custom-call | flops 10000000 | bytes 4000000 | tf_op jit(solution)/shard_map/collect/pallas_call | solution.py:552
  125.4 11.8 %all_to_all.36.refs_8_ = f32[16,8,128]{2,1,0:T(8,128)} all-to-all(f32[16,8,128]{2,1,0:T(8,128)} %get-tuple-element.35), channel_id=1, replica_groups=mesh['seg'=8,'sec'=16] {'sec'}, dimensions={0} | all-to-all | bytes 131072 | tf_op jit(solution)/shard_map/all_to_all | solution.py:610
  137.1 11.9 %apply_first.1 = (f32[8,128,128]{2,1,0:T(8,128)}, f32[8,128,128]{2,1,0:T(8,128)}, f32[8,128,128]{2,1,0:T(8,128)}, bf16[48,128,128]{2,1,0:T(8,128)(2,1)}, f32[8,128,128]{2,1,0:T(8,128)}) custom-call(s32[1]{0:T(128)} %bitcast.2.flag_ref.refs_0_, s32[40]{0:T(128)} %get-tuple-element.28.slot_ref.refs_1_, s32[40]{0:T(128)} %get-tuple-element.29.local_ref.refs_2_, ...), custom_call_target="tpu_custom_call" | custom-call | flops 10000000000 | bytes 10000000 | tf_op jit(solution)/shard_map/apply_first/pallas_call | solution.py:473
  149.1 24.9 %all_to_all.37 = bf16[16,3,128,128]{3,2,1,0:T(8,128)(2,1)} all-to-all(bf16[16,3,128,128]{3,2,1,0:T(8,128)(2,1)} %bitcast.24), channel_id=1, replica_groups=mesh['seg'=8,'sec'=16] {'sec'}, dimensions={0} | all-to-all | bytes 3145728 | tf_op jit(solution)/shard_map/all_to_all | solution.py:610
  173.9 4.8 %collect.4 = (f32[8,128,128]{2,1,0:T(8,128)}, f32[16,8,128]{2,1,0:T(8,128)}) custom-call(s32[40]{0:T(128)} %get-tuple-element.27.refs_0_, s32[8]{0:T(128)} %dynamic_slice.6.left_ref.refs_1_, s32[32]{0:T(128)} %reshape.32.right_ref.refs_2_, bf16[48,128,128]{2,1,0:T(8,128)(2,1)} %bitcast.19, f32[8,128,128]{2,1,0:T(8,128)} %get-tuple-element.38.refs_4_, ...), custom_call_target="tpu_custom_call" | custom-call | flops 10000000 | bytes 4000000 | tf_op jit(solution)/shard_map/collect/pallas_call | solution.py:552
  178.7 11.8 %all_to_all.38.refs_8_ = f32[16,8,128]{2,1,0:T(8,128)} all-to-all(f32[16,8,128]{2,1,0:T(8,128)} %get-tuple-element.42), channel_id=1, replica_groups=mesh['seg'=8,'sec'=16] {'sec'}, dimensions={0} | all-to-all | bytes 131072 | tf_op jit(solution)/shard_map/all_to_all | solution.py:610
  190.5 12.3 %apply_later.1 = (f32[8,128,128]{2,1,0:T(8,128)}, f32[8,128,128]{2,1,0:T(8,128)}, f32[8,128,128]{2,1,0:T(8,128)}, bf16[48,128,128]{2,1,0:T(8,128)(2,1)}, f32[8,128,128]{2,1,0:T(8,128)}) custom-call(s32[1]{0:T(128)} %bitcast.2.flag_ref.refs_0_, s32[40]{0:T(128)} %get-tuple-element.28.slot_ref.refs_1_, s32[40]{0:T(128)} %get-tuple-element.29.local_ref.refs_2_, ...), custom_call_target="tpu_custom_call" | custom-call | flops 10000000000 | bytes 10000000 | tf_op jit(solution)/shard_map/apply_later/pallas_call | solution.py:473
  202.8 22.8 %all_to_all.39 = bf16[16,3,128,128]{3,2,1,0:T(8,128)(2,1)} all-to-all(bf16[16,3,128,128]{3,2,1,0:T(8,128)(2,1)} %bitcast.23), channel_id=1, replica_groups=mesh['seg'=8,'sec'=16] {'sec'}, dimensions={0} | all-to-all | bytes 3145728 | tf_op jit(solution)/shard_map/all_to_all | solution.py:610
  225.6 3.9 %collect.5 = (f32[8,128,128]{2,1,0:T(8,128)}, f32[16,8,128]{2,1,0:T(8,128)}) custom-call(s32[40]{0:T(128)} %get-tuple-element.27.refs_0_, s32[8]{0:T(128)} %dynamic_slice.6.left_ref.refs_1_, s32[32]{0:T(128)} %reshape.32.right_ref.refs_2_, bf16[48,128,128]{2,1,0:T(8,128)(2,1)} %bitcast.17, f32[8,128,128]{2,1,0:T(8,128)} %get-tuple-element.45.refs_4_, ...), custom_call_target="tpu_custom_call" | custom-call | flops 10000000 | bytes 4000000 | tf_op jit(solution)/shard_map/collect/pallas_call | solution.py:552
  229.5 11.8 %all_to_all.40.gram_ref = f32[16,8,128]{2,1,0:T(8,128)} all-to-all(f32[16,8,128]{2,1,0:T(8,128)} %get-tuple-element.49), channel_id=1, replica_groups=mesh['seg'=8,'sec'=16] {'sec'}, dimensions={0} | all-to-all | bytes 131072 | tf_op jit(solution)/shard_map/all_to_all | solution.py:610
  241.3 2.5 %finish.1 = (f32[8,64,256]{2,1,0:T(8,128)}, f32[8,128]{1,0:T(8,128)}) custom-call(f32[16,8,128]{2,1,0:T(8,128)} %all_to_all.40.gram_ref, f32[8,128,128]{2,1,0:T(8,128)} %get-tuple-element.48.refs_7_.x_ref, f32[8,128,128]{2,1,0:T(8,128)} %get-tuple-element.47.refs_6_.d_ref), custom_call_target="tpu_custom_call" | custom-call | flops 1000000 | bytes 2000000 | tf_op jit(solution)/shard_map/finish/pallas_call | solution.py:591
  (25 shorter events, 7.8 us)
Async XLA Ops:
  0.6 62.3 %copy-start = (s32[128,4]{0,1:T(4,128)S(1)}, s32[128,4]{0,1:T(4,128)}, u32[]{:S(2)}) copy-start(s32[128,4]{0,1:T(4,128)} %param.19) | copy-start | bytes 6148
  9.8 8.3 %copy-start.1 = (bf16[1,8,64,1920]{3,2,1,0:T(8,128)(2,1)S(1)}, bf16[1,8,64,1920]{3,2,1,0:T(8,128)(2,1)}, u32[]{:S(2)}) copy-start(bf16[1,8,64,1920]{3,2,1,0:T(8,128)(2,1)} %param.11) | copy-start | bytes 5898244
  9.8 10.2 %copy-start.3 = (s32[30,30]{1,0:T(8,128)S(1)}, s32[30,30]{1,0:T(8,128)}, u32[]{:S(2)}) copy-start(s32[30,30]{1,0:T(8,128)} %param.16) | copy-start | bytes 10804
  9.8 10.2 %copy-start.2 = (bf16[30,4,30,4]{2,3,1,0:T(4,128)(2,1)S(1)}, bf16[30,4,30,4]{2,3,1,0:T(4,128)(2,1)}, u32[]{:S(2)}) copy-start(bf16[30,4,30,4]{2,3,1,0:T(4,128)(2,1)} %param.15) | copy-start | bytes 86404
  9.8 32.8 %all-to-all-start = ((bf16[16,3,64,256]{3,2,1,0:T(8,128)(2,1)}), bf16[16,3,64,256]{3,2,1,0:T(8,128)(2,1)}, u32[]{:S(2)}, u32[]{:S(2)}) async-start(bf16[16,3,64,256]{3,2,1,0:T(8,128)(2,1)} %get-tuple-element.30), calls=%async_computation | async-start | bytes 3145728 | tf_op jit(solution)/shard_map/all_to_all | solution.py:610
  18.1 49.0 %collective-permute-start = (bf16[8,64,1920]{2,1,0:T(8,128)(2,1)S(1)}, bf16[8,64,1920]{2,1,0:T(8,128)(2,1)}, u32[]{:S(2)}, u32[]{:S(2)}) collective-permute-start(bf16[8,64,1920]{2,1,0:T(8,128)(2,1)S(1)} %bitcast.22), channel_id=1, source_target_pairs={{16,0},{32,16},{48,32},{64,48},{80,64},{96,80},{112,96},{17,1},{33... | collective-permute-start | bytes 5898248 | tf_op jit(solution)/shard_map/ppermute | solution.py:31
  49.7 12.6 %copy-start.5 = (s32[128]{0:T(128)S(1)}, s32[128]{0:T(128)}, u32[]{:S(2)}) copy-start(s32[128]{0:T(128)} %param.18) | copy-start | bytes 1540
  56.8 15.9 %collective-permute-start.1 = (bf16[4,960,128]{2,1,0:T(8,128)(2,1)}, bf16[4,960,128]{2,1,0:T(8,128)(2,1)S(1)}, u32[]{:S(2)}, u32[]{:S(2)}) collective-permute-start(bf16[4,960,128]{2,1,0:T(8,128)(2,1)} %build_environment.2), channel_id=1, source_target_pairs={{0,16},{16,32},{32,48},{48,64},{64,80},{80,96},{96,112},{1,17},{17... | collective-permute-start | bytes 2949128 | tf_op jit(solution)/shard_map/ppermute | solution.py:31
  58.8 24.3 %collective-permute-start.2 = (bf16[4,960,128]{2,1,0:T(8,128)(2,1)}, bf16[4,960,128]{2,1,0:T(8,128)(2,1)}, u32[]{:S(2)}, u32[]{:S(2)}) collective-permute-start(bf16[4,960,128]{2,1,0:T(8,128)(2,1)} %build_environment.3), channel_id=1, source_target_pairs={{0,16},{16,32},{32,48},{48,64},{64,80},{80,96},{96,112},{1,17},{17... | collective-permute-start | bytes 2949128 | tf_op jit(solution)/shard_map/ppermute | solution.py:31
  72.8 10.3 %copy-start.4 = (bf16[4,960,128]{2,1,0:T(8,128)(2,1)}, bf16[4,960,128]{2,1,0:T(8,128)(2,1)S(1)}, u32[]{:S(2)}) copy-start(bf16[4,960,128]{2,1,0:T(8,128)(2,1)S(1)} %collective-permute-done.1.refs_6_) | copy-start | bytes 2949124

commit v4 on v3

--- a/solution.py
+++ b/solution.py
@@ -14,6 +14,7 @@
 CLASSES = 5
 GROUP = W // CLASSES
 PAIRS = SEC_DEV * CLASSES
+SHIFT = SEC_DEV.bit_length() - 1
 HALF = B // 2
 FOLD = 2 * B
 ROWS = W * HALF
@@ -76,41 +77,37 @@
     return jnp.dot(left, right, preferred_element_type=F32)
 
 
-def route_kernel(me_ref, shift_ref, site_ref, slot_ref, local_ref, take_ref, send_ref, count, source):
+def route_kernel(me_ref, shift_ref, source_ref, site_ref, slot_ref, local_ref, take_ref, send_ref, count, source):
     groups = send_ref.shape[0]
     slots = send_ref.shape[1]
     me = me_ref[0]
     for g in range(groups):
         count[g] = 0
+        count[groups + g] = 0
     for i in range(groups * slots):
         source[i] = 0
-    for l in range(SEC_DEV):
-        for k in range(CLASSES):
-            target = shift_ref[k, me * SEC_DEV + l]
-            owner = target // SEC_DEV
-            rank = count[owner]
-            count[owner] = rank + 1
-            slot_ref[l * CLASSES + k] = owner * slots + jnp.minimum(rank, slots - 1)
-            local_ref[l * CLASSES + k] = jnp.where(owner == me, target % SEC_DEV, -1)
-
-    def one_group(g, carry):
-        rank = jnp.int32(0)
+    for k in range(CLASSES):
+        targets = [shift_ref[k, me * SEC_DEV + l] for l in range(SEC_DEV)]
+        owners = [target >> SHIFT for target in targets]
+        ranks = [count[owner] for owner in owners]
+        for one in range(SEC_DEV):
+            for two in range(one):
+                same = owners[one] == owners[two]
+                above = targets[one] > targets[two]
+                ranks[one] = ranks[one] + (same & above).astype(jnp.int32)
+                ranks[two] = ranks[two] + (same & jnp.logical_not(above)).astype(jnp.int32)
         for l in range(SEC_DEV):
-            for k in range(CLASSES):
-                target = shift_ref[k, g * SEC_DEV + l]
-                hit = target // SEC_DEV == me
-                place = jnp.minimum(rank, slots - 1)
-
-                @pl.when(hit)
-                def _():
-                    local = target % SEC_DEV
-                    take_ref[k * SEC_DEV + local] = jnp.where(g == me, -1, g * slots + place)
-                    source[g * slots + place] = local
-
-                rank = rank + hit.astype(jnp.int32)
-        return carry
-
-    lax.fori_loop(0, groups, one_group, 0)
+            slot_ref[l * CLASSES + k] = owners[l] * slots + jnp.minimum(ranks[l], slots - 1)
+            local_ref[l * CLASSES + k] = jnp.where(owners[l] == me, targets[l] & (SEC_DEV - 1), -1)
+        for owner in owners:
+            count[owner] = count[owner] + 1
+        for m in range(SEC_DEV):
+            g = source_ref[k, m] >> SHIFT
+            rank = count[groups + g]
+            count[groups + g] = rank + 1
+            place = g * slots + jnp.minimum(rank, slots - 1)
+            take_ref[k * SEC_DEV + m] = jnp.where(g == me, -1, place)
+            source[place] = m
 
     def one_copy(g, carry):
         for r in range(slots):
@@ -121,6 +118,10 @@
 
 
 def route(me, sector_shift, site, groups, slots):
+    mine = me * SEC_DEV + jnp.arange(SEC_DEV, dtype=jnp.int32)
+    sector = jnp.arange(sector_shift.shape[1], dtype=jnp.int32)
+    hit = sector_shift[:, None, :] == mine[None, :, None]
+    source = jnp.sum(jnp.where(hit, sector[None, None, :], 0), axis=2)
     smem = pl.BlockSpec(memory_space=pltpu.SMEM)
     vmem = pl.BlockSpec(memory_space=pltpu.VMEM)
     return pl.pallas_call(
@@ -131,11 +132,14 @@
             jax.ShapeDtypeStruct((PAIRS,), jnp.int32),
             jax.ShapeDtypeStruct((groups, slots, B, D * B), BF),
         ),
-        in_specs=[smem, smem, vmem],
+        in_specs=[smem, smem, smem, vmem],
         out_specs=(smem, smem, smem, vmem),
-        scratch_shapes=[pltpu.SMEM((groups,), jnp.int32), pltpu.SMEM((groups * slots,), jnp.int32)],
+        scratch_shapes=[
+            pltpu.SMEM((2 * groups,), jnp.int32),
+            pltpu.SMEM((groups * slots,), jnp.int32),
+        ],
         name="route",
-    )(me, sector_shift, site)
+    )(me[None], sector_shift, source, site)
 
 
 def fold_environment_kernel(flag_ref, *refs):
@@ -376,81 +380,41 @@
     return (cosine, sine) + correction_scalars(*named)
 
 
-def apply_kernel(mode, entries, *refs):
-    flag_ref, slot_ref, local_ref, mix_ref, right_ref, left_ref, early_ref, late_ref = refs[:8]
-    refs = refs[8:]
-    step_at = pl.program_id(0)
-    if mode == "start":
-        state_ref, send_ref, own_ref = refs[:3]
-        scratch = refs[3:]
-    elif mode == "first":
-        gram_ref, u_ref, h_ref, weight_ref = refs[:4]
-        x_out, a_out, d_out, send_ref, own_ref = refs[4:9]
-        scratch = refs[9:]
-    else:
-        gram_ref, x_ref, a_ref, d_ref, p_ref, weight_ref = refs[:6]
-        x_out, a_out, d_out, send_ref, own_ref = refs[6:11]
-        scratch = refs[11:]
-    fixed, partials = scratch[:2]
-    scratch = scratch[2:]
-    size = right_ref.shape[0]
-
-    @pl.when(step_at == 0)
-    def _():
-        own_ref[...] = jnp.zeros_like(own_ref)
-        for first in scratch[:size]:
-            first[W * D * PITCH :, :] = jnp.zeros(((MIX - W * D) * PITCH, FOLD), F32)
-        if mode != "start":
-            scalars = first_scalars if mode == "first" else later_scalars
-            for i, value in enumerate(scalars(gram_ref, entries)):
-                fixed[i : i + 1, :] = jnp.broadcast_to(value, (1, FOLD))
-
-    for n in range(size):
-        first = scratch[n]
-        if mode == "start":
-            vector = state_ref[n]
-        else:
-            if mode == "first":
-                inverse, rho, along, norm = [fixed[i : i + 1, :] for i in range(4)]
-                current = inverse * u_ref[n]
-                applied = inverse * h_ref[n]
-            else:
-                cosine, sine, rho, along, norm = [fixed[i : i + 1, :] for i in range(5)]
-                current = cosine * x_ref[n] + sine * d_ref[n]
-                applied = cosine * a_ref[n] + sine * p_ref[n]
-            vector = (weight_ref[n] * (applied - rho * current) - along * current) * norm
-            x_out[n] = current
-            a_out[n] = applied
-            d_out[n] = vector
-        right = jnp.concatenate(
-            [spread(vector[s * HALF : (s + 1) * HALF]) for s in range(D)], axis=1
-        ).astype(BF)
-        rows = GROUP * HALF
-        for i in range(CLASSES):
-            product = dot(right_ref[n, i * rows : (i + 1) * rows, :], right)
-            for v in range(GROUP):
-                for s in range(D):
-                    at = ((i * GROUP + v) * D + s) * PITCH
-                    first[at : at + HALF, :] = product[v * HALF : (v + 1) * HALF, s * FOLD : (s + 1) * FOLD]
-    for n in range(size):
-        mix_channels(mix_ref[...], scratch[n], scratch[size + n])
-    own_left = flag_ref[0] == 1
-    early = step_at < SEC_DEV // 2 // size
+def clear_padding(scratch):
+    for first in scratch:
+        first[W * D * PITCH :, :] = jnp.zeros(((MIX - W * D) * PITCH, FOLD), F32)
+
+
+def contract_right(vector, right_ref, n, first):
+    right = jnp.concatenate([spread(vector[s * HALF : (s + 1) * HALF]) for s in range(D)], axis=1).astype(BF)
+    rows = GROUP * HALF
+    for i in range(CLASSES):
+        product = dot(right_ref[n, i * rows : (i + 1) * rows, :], right)
+        for v in range(GROUP):
+            for s in range(D):
+                at = ((i * GROUP + v) * D + s) * PITCH
+                first[at : at + HALF, :] = product[v * HALF : (v + 1) * HALF, s * FOLD : (s + 1) * FOLD]
+
+
+def contract_left(n, own_left, early, left_refs, rows_of, at, slot_ref, send_ref, partials):
+    left_ref, early_ref, late_ref = left_refs
+    for k in range(CLASSES):
+        rows, blocks = [], []
+        for w in range(k * GROUP, (k + 1) * GROUP):
+            part = slice(w * HALF, (w + 1) * HALF)
+            handed = jnp.where(early, early_ref[n, part, :], late_ref[n, part, :])
+            chosen = jnp.where(own_left, left_ref[n, part, :], handed)
+            rows.append(rows_of(w))
+            blocks.append(spread(chosen.astype(F32)).astype(BF))
+        partial = dot(jnp.concatenate(rows, axis=1), jnp.concatenate(blocks, axis=0))
+        partials[n * CLASSES + k] = partial
+        send_ref[slot_ref[at * CLASSES + k]] = partial.astype(BF)
+
+
+def add_own(base, size, local_ref, own_ref, partials):
     for n in range(size):
         for k in range(CLASSES):
-            rows, blocks = [], []
-            for w in range(k * GROUP, (k + 1) * GROUP):
-                at = slice(w * HALF, (w + 1) * HALF)
-                handed = jnp.where(early, early_ref[n, at, :], late_ref[n, at, :])
-                chosen = jnp.where(own_left, left_ref[n, at, :], handed)
-                rows.append(mixed_rows(scratch[size + n], w))
-                blocks.append(spread(chosen.astype(F32)).astype(BF))
-            partial = dot(jnp.concatenate(rows, axis=1), jnp.concatenate(blocks, axis=0))
-            partials[n * CLASSES + k] = partial
-            send_ref[slot_ref[(step_at * size + n) * CLASSES + k]] = partial.astype(BF)
-    for n in range(size):
-        for k in range(CLASSES):
-            local = local_ref[(step_at * size + n) * CLASSES + k]
+            local = local_ref[(base + n) * CLASSES + k]
 
             @pl.when(local >= 0)
             def _():
@@ -458,7 +422,98 @@
                 own_ref[place] = own_ref[place] + partials[n * CLASSES + k]
 
 
-def apply_operator(mode, entries, slots_total, flag, slot, local, mix, right_env, left_envs, gram, vectors):
+def mix_start_kernel(mix_ref, right_ref, state_ref, out_ref, *scratch):
+    size = right_ref.shape[0]
+
+    @pl.when(pl.program_id(0) == 0)
+    def _():
+        clear_padding(scratch[:size])
+
+    for n in range(size):
+        contract_right(state_ref[n], right_ref, n, scratch[n])
+    for n in range(size):
+        mix_channels(mix_ref[...], scratch[n], scratch[size + n])
+    for n in range(size):
+        for w in range(W):
+            out_ref[n, w * TILE : (w + 1) * TILE, :] = mixed_rows(scratch[size + n], w)
+
+
+def mix_start(mix, right_env, start):
+    step = 2
+    block = lambda rows: pl.BlockSpec((step, rows, FOLD), lambda l: (l, 0, 0))
+    return pl.pallas_call(
+        mix_start_kernel,
+        grid=(SEC_DEV // step,),
+        out_shape=jax.ShapeDtypeStruct((SEC_DEV, W * TILE, FOLD), BF),
+        in_specs=[pl.BlockSpec(mix.shape, lambda l: (0, 0)), block(ROWS), block(TILE)],
+        out_specs=block(W * TILE),
+        scratch_shapes=[pltpu.VMEM((MIX * PITCH, FOLD), F32)] * (2 * step),
+        name="mix_start",
+        cost_estimate=pl.CostEstimate(flops=10**10, bytes_accessed=10**7, transcendentals=0),
+    )(mix, right_env, start)
+
+
+def join_start_kernel(flag_ref, slot_ref, local_ref, mixed_ref, *refs):
+    left_refs, (send_ref, own_ref, partials) = refs[:3], refs[3:]
+    size = mixed_ref.shape[0]
+    base = pl.program_id(0) * size
+
+    @pl.when(base == 0)
+    def _():
+        own_ref[...] = jnp.zeros_like(own_ref)
+
+    own_left = flag_ref[0] == 1
+    early = base < SEC_DEV // 2
+    for n in range(size):
+        rows_of = lambda w: mixed_ref[n, w * TILE : (w + 1) * TILE, :]
+        contract_left(n, own_left, early, left_refs, rows_of, base + n, slot_ref, send_ref, partials)
+    add_own(base, size, local_ref, own_ref, partials)
+
+
+def apply_kernel(mode, entries, *refs):
+    flag_ref, slot_ref, local_ref, mix_ref, right_ref = refs[:5]
+    left_refs = refs[5:8]
+    inputs = refs[8 : 12 if mode == "first" else 14]
+    x_out, a_out, d_out, send_ref, own_ref, fixed, partials = refs[8 + len(inputs) : 15 + len(inputs)]
+    scratch = refs[15 + len(inputs) :]
+    size = right_ref.shape[0]
+    base = pl.program_id(0) * size
+
+    @pl.when(base == 0)
+    def _():
+        own_ref[...] = jnp.zeros_like(own_ref)
+        clear_padding(scratch[:size])
+        scalars = first_scalars if mode == "first" else later_scalars
+        for i, value in enumerate(scalars(inputs[0], entries)):
+            fixed[i : i + 1, :] = jnp.broadcast_to(value, (1, FOLD))
+
+    for n in range(size):
+        if mode == "first":
+            u_ref, h_ref, weight_ref = inputs[1:]
+            inverse, rho, along, norm = [fixed[i : i + 1, :] for i in range(4)]
+            current = inverse * u_ref[n]
+            applied = inverse * h_ref[n]
+        else:
+            x_ref, a_ref, d_ref, p_ref, weight_ref = inputs[1:]
+            cosine, sine, rho, along, norm = [fixed[i : i + 1, :] for i in range(5)]
+            current = cosine * x_ref[n] + sine * d_ref[n]
+            applied = cosine * a_ref[n] + sine * p_ref[n]
+        vector = (weight_ref[n] * (applied - rho * current) - along * current) * norm
+        x_out[n] = current
+        a_out[n] = applied
+        d_out[n] = vector
+        contract_right(vector, right_ref, n, scratch[n])
+    for n in range(size):
+        mix_channels(mix_ref[...], scratch[n], scratch[size + n])
+    own_left = flag_ref[0] == 1
+    early = base < SEC_DEV // 2
+    for n in range(size):
+        rows_of = functools.partial(mixed_rows, scratch[size + n])
+        contract_left(n, own_left, early, left_refs, rows_of, base + n, slot_ref, send_ref, partials)
+    add_own(base, size, local_ref, own_ref, partials)
+
+
+def apply_operator(mode, entries, slots_total, tables, left_envs, fixed_inputs, vectors):
     step = 2
     halves = SEC_DEV // step // 2
     vector = pl.BlockSpec((step, TILE, FOLD), lambda l, *refs: (l, 0, 0))
@@ -467,25 +522,34 @@
     late = pl.BlockSpec((step, ROWS, FOLD), lambda l, *refs: (jnp.maximum(l - halves, 0), 0, 0))
     whole = lambda shape: pl.BlockSpec(shape, lambda l, *refs: (0,) * len(shape))
     shape = jax.ShapeDtypeStruct((SEC_DEV, TILE, FOLD), F32)
-    kept = 0 if mode == "start" else 3
     send = jax.ShapeDtypeStruct((slots_total, TILE, FOLD), BF)
-    inputs = (mix, right_env) + tuple(left_envs) + (() if gram is None else (gram,)) + tuple(vectors)
+    lefts = [folded, early, late]
+    partials = [pltpu.VMEM((step * CLASSES, TILE, FOLD), F32)]
+    if mode == "start":
+        kernel, kept = join_start_kernel, 0
+        (mixed,) = fixed_inputs
+        inputs = (mixed, *left_envs)
+        in_specs = [pl.BlockSpec((step, W * TILE, FOLD), lambda l, *refs: (l, 0, 0))] + lefts
+        scratch = partials
+    else:
+        kernel, kept = functools.partial(apply_kernel, mode, entries), 3
+        mix, right_env, gram = fixed_inputs
+        inputs = (mix, right_env, *left_envs, gram, *vectors)
+        in_specs = [whole(mix.shape), folded] + lefts + [whole(gram.shape)] + [vector] * len(vectors)
+        scratch = [pltpu.VMEM((8, FOLD), F32)] + partials
+        scratch += [pltpu.VMEM((MIX * PITCH, FOLD), F32)] * (2 * step)
     return pl.pallas_call(
-        functools.partial(apply_kernel, mode, entries),
+        kernel,
         out_shape=(shape,) * kept + (send, shape),
         grid_spec=pltpu.PrefetchScalarGridSpec(
             num_scalar_prefetch=3,
             grid=(SEC_DEV // step,),
-            in_specs=[whole(mix.shape), folded, folded, early, late]
-            + ([] if gram is None else [whole(gram.shape)])
-            + [vector] * len(vectors),
+            in_specs=in_specs,
             out_specs=(vector,) * kept + (whole(send.shape), whole(shape.shape)),
-            scratch_shapes=[pltpu.VMEM((8, FOLD), F32), pltpu.VMEM((step * CLASSES, TILE, FOLD), F32)]
-            + [pltpu.VMEM((MIX * PITCH, FOLD), F32)] * (2 * step),
-        ),
-        name="apply_" + mode,
+            scratch_shapes=scratch,
+        ),
         cost_estimate=pl.CostEstimate(flops=10**10, bytes_accessed=10**7, transcendentals=0),
-    )(flag, slot, local, *inputs)
+    )(*tables, *inputs)
 
 
 def collect_kernel(names, *refs):
@@ -575,7 +639,7 @@
         energy = cosine * cosine * xa + cosine * sine * (xp + da) + sine * sine * dp
         fixed[0:1, :] = jnp.broadcast_to(cosine, (1, FOLD))
         fixed[1:2, :] = jnp.broadcast_to(sine, (1, FOLD))
-        energy_ref[...] = jnp.broadcast_to(energy, energy_ref.shape)
+        energy_ref[0] = jnp.sum(energy)
 
     for n in range(x_ref.shape[0]):
         final = fixed[0:1, :] * x_ref[n] + fixed[1:2, :] * d_ref[n]
@@ -593,12 +657,12 @@
         grid=(SEC_DEV // step,),
         out_shape=(
             jax.ShapeDtypeStruct((SEC_DEV, B, D * B), F32),
-            jax.ShapeDtypeStruct((8, FOLD), F32),
+            jax.ShapeDtypeStruct((1,), F32),
         ),
         in_specs=[pl.BlockSpec(gram.shape, lambda l: (0, 0, 0)), vector, vector],
         out_specs=(
             pl.BlockSpec((step, B, D * B), lambda l: (l, 0, 0)),
-            pl.BlockSpec((8, FOLD), lambda l: (0, 0)),
+            pl.BlockSpec(memory_space=pltpu.SMEM),
         ),
         scratch_shapes=[pltpu.VMEM((8, FOLD), F32)],
         name="finish",
@@ -635,26 +699,28 @@
     at_end = (position == last).astype(jnp.int32)[None]
     at_start = (position == 0).astype(jnp.int32)[None]
     came_right = passed_along(right_environment[0], "seg", -1)
-
-    slot, local, take, site_send = route(my_group[None], sector_shift, site_previous[0], groups, slots)
+    slot, local, take, site_send = route(my_group, sector_shift, site_previous[0], groups, slots)
     site_came = exchange(site_send).reshape(groups * slots, B, D * B)
     mix = channel_tensor * channel_mask.astype(BF)[:, None, :, None]
     mix = jnp.pad(mix.reshape(W * D, W * D), ((0, MIX - W * D), (0, MIX - W * D)))
-
     own_left = fold_environment(at_start, left_environment[0])
+    start, weight = fold_state(my_left, my_right, state_start[0], preconditioner[0])
+    right_env = fold_environment(at_end, right_environment[0], came_right)
     handed = []
+    sectors = SEC_DEV // 2
     for half in range(2):
-        sectors = SEC_DEV // 2
         fresh = build_environment(
             half * sectors, sectors, slot, local, own_left, site_previous[0], site_came, mix
         )
         handed.append(passed_along(fresh, "seg", 1))
-    right_env = fold_environment(at_end, right_environment[0], came_right)
-    start, weight = fold_state(my_left, my_right, state_start[0], preconditioner[0])
+    mixed = mix_start(mix, right_env, start)
 
     apply = functools.partial(
-        apply_operator, entries=entries, slots_total=groups * slots, flag=at_start, slot=slot, local=local,
-        mix=mix, right_env=right_env, left_envs=(own_left, *handed),
+        apply_operator,
+        entries=entries,
+        slots_total=groups * slots,
+        tables=(at_start, slot, local),
+        left_envs=(own_left, *handed),
     )
 
     def gather(names, send, own, vectors, weight):
@@ -662,16 +728,20 @@
         result, gram = collect(names, groups, take, my_left, my_right, came, own, vectors, weight)
         return result, exchange(gram)
 
-    send, own = apply("start", gram=None, vectors=(start,))
+    send, own = apply("start", fixed_inputs=(mixed,), vectors=())
     product, gram = gather(FIRST, send, own, (start,), weight)
-    current, applied, direction, send, own = apply("first", gram=gram, vectors=(start, product, weight))
+    current, applied, direction, send, own = apply(
+        "first", fixed_inputs=(mix, right_env, gram), vectors=(start, product, weight)
+    )
     product, gram = gather(LATER, send, own, (applied, direction, current), weight)
     current, applied, direction, send, own = apply(
-        "later", gram=gram, vectors=(current, applied, direction, product, weight)
+        "later",
+        fixed_inputs=(mix, right_env, gram),
+        vectors=(current, applied, direction, product, weight),
     )
     product, gram = gather(LAST, send, own, (applied, direction, current), None)
     state, energy = finish(entries, gram, current, direction)
-    return (state[None], energy[0, :1])
+    return (state[None], energy)
 
 
 def solution(mesh):
@@ -688,6 +758,4 @@
         P(),
     )
     out_specs = (P("seg", "sec", None, None), P("seg"))
-    return jax.shard_map(
-        on_device, mesh=mesh, in_specs=in_specs, out_specs=out_specs, check_vma=False
-    )
+    return jax.shard_map(on_device, mesh=mesh, in_specs=in_specs, out_specs=out_specs, check_vma=False)

time: 246 us -> 239 us (0.972)
  waiting for transfers between devices: 24.2 us -> 13.9 us
    ppermute x3, waiting for transfers between devices: 10.3 us -> 0.01 us  [passed_along(): return lax.ppermute(block, axis, route)]
    pallas_call x1, Pallas kernels: 9.13 us -> 3.33 us  [route(): pl.pallas_call(route_kernel, out_shape=(jax.ShapeDtypeStruct((PAIRS,), jn...]
    pallas_call x3 -> x4, Pallas kernels: 35.8 us -> 41 us  [the longest x3 32.6 us: apply_operator(): pl.pallas_call(kernel, out_shape=(shape,) * kept + (send, shape), grid_sp...]
  transfers between devices with their start and end apart: 4 -> 4, of which waited for: 2 -> 1; matrix products, arithmetic and copies ran while one was open for 2% -> 2% of each run, Pallas kernels for 12% -> 15%
where the time goes in v4:
time: 239 us; the launch traced here: 238 us
  blocking collectives  112 us (47%)
  Pallas kernels  88.2 us (37%)
  starting transfers between devices  15.9 us (7%)
  waiting for transfers between devices  13.9 us (6%)
  local copies, waits for them, and re-layouts  5.68 us (2%)
    all_to_all x6, blocking collectives, exchange(): return lax.all_to_all(blocks, 'sec', 0, 0, tiled=True)  112 us
    pallas_call x3, Pallas kernels, apply_operator(): pl.pallas_call(kernel, out_shape=(shape,) * kept + (send, shape), grid_sp...  32.6 us
    pallas_call x2, Pallas kernels, build_environment(): pl.pallas_call(functools.partial(build_kernel, half), out_shape=jax.Shape...  14 us
    all_to_all x1, waiting for transfers between devices, exchange(): return lax.all_to_all(blocks, 'sec', 0, 0, tiled=True)  13.9 us
    pallas_call x3, Pallas kernels, collect(): pl.pallas_call(functools.partial(collect_kernel, names), out_shape=(jax.S...  12.7 us
    pallas_call x2, Pallas kernels, fold_environment(): pl.pallas_call(fold_environment_kernel, out_shape=jax.ShapeDtypeStruct((S...  11 us
    pallas_call x1, Pallas kernels, mix_start(): pl.pallas_call(mix_start_kernel, grid=(SEC_DEV // step,), out_shape=jax.S...  8.34 us
    all_to_all x1, starting transfers between devices, exchange(): return lax.all_to_all(blocks, 'sec', 0, 0, tiled=True)  8.24 us
  transfers between devices with their start and end apart: 4, of which 1 were waited for; matrix products, arithmetic and copies ran while one was open for 2% of the time, Pallas kernels for 15%

profile of v4, /device:TPU:2, one launch (start us, length us, event | category | flops | bytes accessed | tf_op | source)
XLA Modules:
  0.0 237.9 jit_solution(10860855059849124675)
XLA Ops:
  2.2 3.3 %route.1 = (s32[40]{0:T(128)}, s32[40]{0:T(128)}, s32[40]{0:T(128)}, bf16[16,3,64,256]{3,2,1,0:T(8,128)(2,1)}) custom-call(s32[1]{0:T(128)} %bitcast.me_ref, s32[5,128]{1,0:T(8,128)} %shift_ref.1, s32[5,8]{1,0:T(8,128)} %select_reduce_fusion.source_ref, bf16[8,64,256]{2,1,0:T(8,128)(2,1)} %bitcast.27), custom_call_target="tpu_custom_call" | custom-call | tf_op jit(solution)/shard_map/route/pallas_call | solution.py:127
  5.6 8.2 %all-to-all-start = ((bf16[16,3,64,256]{3,2,1,0:T(8,128)(2,1)}), bf16[16,3,64,256]{3,2,1,0:T(8,128)(2,1)}, u32[]{:S(2)}, u32[]{:S(2)}) async-start(bf16[16,3,64,256]{3,2,1,0:T(8,128)(2,1)} %get-tuple-element.30), calls=%async_computation | async-start | bytes 3145728 | tf_op jit(solution)/shard_map/all_to_all | solution.py:674
  19.2 5.4 %fold_environment.3.env_ref.refs_0_.refs_5_ = bf16[8,960,128]{2,1,0:T(8,128)(2,1)} custom-call(s32[1]{0:T(128)} %bitcast.2.flag_ref.refs_0_, bf16[8,64,1920]{2,1,0:T(8,128)(2,1)} %bitcast.19), custom_call_target="tpu_custom_call" | custom-call | bytes 3932160 | tf_op jit(solution)/shard_map/fold_environment/pallas_call | solution.py:158
  24.5 13.9 %all-to-all-done = bf16[16,3,64,256]{3,2,1,0:T(8,128)(2,1)} async-done(((bf16[16,3,64,256]{3,2,1,0:T(8,128)(2,1)}), bf16[16,3,64,256]{3,2,1,0:T(8,128)(2,1)}, u32[]{:S(2)}, u32[]{:S(2)}) %all-to-all-start) | async-done | bytes 1572896 | tf_op jit(solution)/shard_map/all_to_all | solution.py:674
  38.4 7.0 %build_environment.2 = bf16[4,960,128]{2,1,0:T(8,128)(2,1)} custom-call(s32[40]{0:T(128)} %get-tuple-element.28.slot_ref.refs_1_, s32[40]{0:T(128)} %get-tuple-element.29.local_ref.refs_2_, bf16[8,960,128]{2,1,0:T(8,128)(2,1)} %fold_environment.3.env_ref.refs_0_.refs_5_, bf16[8,64,256]{2,1,0:T(8,128)(2,1)} %bitcast.28, ...), custom_call_target="tpu_custom_call" | custom-call | flops 10000000000 | bytes 10000000 | tf_op jit(solution)/shard_map/build_environment/pallas_call | solution.py:283
  45.4 2.0 collective-permute-start.1
  47.4 7.0 %build_environment.3 = bf16[4,960,128]{2,1,0:T(8,128)(2,1)} custom-call(s32[40]{0:T(128)} %get-tuple-element.28.slot_ref.refs_1_, s32[40]{0:T(128)} %get-tuple-element.29.local_ref.refs_2_, bf16[8,960,128]{2,1,0:T(8,128)(2,1)} %fold_environment.3.env_ref.refs_0_.refs_5_, bf16[8,64,256]{2,1,0:T(8,128)(2,1)} %bitcast.29, ...), custom_call_target="tpu_custom_call" | custom-call | flops 10000000000 | bytes 10000000 | tf_op jit(solution)/shard_map/build_environment/pallas_call | solution.py:283
  54.5 3.7 %collective-permute-start.2 = (bf16[4,960,128]{2,1,0:T(8,128)(2,1)}, bf16[4,960,128]{2,1,0:T(8,128)(2,1)}, u32[]{:S(2)}, u32[]{:S(2)}) collective-permute-start(bf16[4,960,128]{2,1,0:T(8,128)(2,1)} %build_environment.3), channel_id=1, source_target_pairs={{0,16},{16,32},{32,48},{48,64},{64,80},{80,96},{96,112},{1,17},{17... | collective-permute-start | bytes 2949128 | tf_op jit(solution)/shard_map/ppermute | solution.py:32
  59.6 3.5 %fold_state.1 = (f32[8,128,128]{2,1,0:T(8,128)}, f32[8,128,128]{2,1,0:T(8,128)}) custom-call(s32[8]{0:T(128)} %dynamic_slice.6.left_ref.refs_1_, s32[32]{0:T(128)} %reshape.37.right_ref.refs_2_, f32[8,64,256]{2,1,0:T(8,128)} %bitcast.25, f32[8,64,256]{2,1,0:T(8,128)} %bitcast.26), custom_call_target="tpu_custom_call" | custom-call | bytes 2097152 | tf_op jit(solution)/shard_map/fold_state/pallas_call | solution.py:201
  63.0 5.7 %fold_environment.2.right_ref.refs_4_ = bf16[8,960,128]{2,1,0:T(8,128)(2,1)} custom-call(s32[1]{0:T(128)} %bitcast.3.flag_ref, bf16[8,64,1920]{2,1,0:T(8,128)(2,1)} %bitcast.20, bf16[8,64,1920]{2,1,0:T(8,128)(2,1)} %collective-permute-done.refs_1_), custom_call_target="tpu_custom_call" | custom-call | bytes 3932160 | tf_op jit(solution)/shard_map/fold_environment/pallas_call | solution.py:158
  68.7 8.3 %mix_start.1.mixed_ref = bf16[8,3840,128]{2,1,0:T(8,128)(2,1)} custom-call(bf16[128,128]{1,0:T(8,128)(2,1)} %pad.4.mix_ref.refs_3_, bf16[8,960,128]{2,1,0:T(8,128)(2,1)} %fold_environment.2.right_ref.refs_4_, f32[8,128,128]{2,1,0:T(8,128)} %get-tuple-element.31.state_ref.refs_5_.refs_9_), custom_call_target="tpu_custom_call" | custom-call | flops 10000000000 | bytes 10000000 | tf_op jit(solution)/shard_map/mix_start/pallas_call | solution.py:444
  78.0 8.5 %shard_map.113 = (bf16[48,128,128]{2,1,0:T(8,128)(2,1)}, f32[8,128,128]{2,1,0:T(8,128)}) custom-call(s32[1]{0:T(128)} %bitcast.2.flag_ref.refs_0_, s32[40]{0:T(128)} %get-tuple-element.28.slot_ref.refs_1_, s32[40]{0:T(128)} %get-tuple-element.29.local_ref.refs_2_, bf16[8,3840,128]{2,1,0:T(8,128)(2,1)} %mix_start.1.mixed_ref, ...), custom_call_target="tpu_custom_call" | custom-call | flops 10000000000 | bytes 10000000 | tf_op jit(solution)/shard_map/pallas_call | solution.py:541
  86.5 27.6 %all_to_all.35 = bf16[16,3,128,128]{3,2,1,0:T(8,128)(2,1)} all-to-all(bf16[16,3,128,128]{3,2,1,0:T(8,128)(2,1)} %bitcast.24), channel_id=1, replica_groups=mesh['seg'=8,'sec'=16] {'sec'}, dimensions={0} | all-to-all | bytes 3145728 | tf_op jit(solution)/shard_map/all_to_all | solution.py:674
  114.1 4.0 %collect.3 = (f32[8,128,128]{2,1,0:T(8,128)}, f32[16,8,128]{2,1,0:T(8,128)}) custom-call(s32[40]{0:T(128)} %get-tuple-element.27.refs_0_, s32[8]{0:T(128)} %dynamic_slice.6.left_ref.refs_1_, s32[32]{0:T(128)} %reshape.37.right_ref.refs_2_, bf16[48,128,128]{2,1,0:T(8,128)(2,1)} %bitcast.17, f32[8,128,128]{2,1,0:T(8,128)} %get-tuple-element.33.refs_4_, ...), custom_call_target="tpu_custom_call" | custom-call | flops 10000000 | bytes 4000000 | tf_op jit(solution)/shard_map/collect/pallas_call | solution.py:616
  118.1 11.8 %all_to_all.36.refs_8_ = f32[16,8,128]{2,1,0:T(8,128)} all-to-all(f32[16,8,128]{2,1,0:T(8,128)} %get-tuple-element.35), channel_id=1, replica_groups=mesh['seg'=8,'sec'=16] {'sec'}, dimensions={0} | all-to-all | bytes 131072 | tf_op jit(solution)/shard_map/all_to_all | solution.py:674
  129.9 11.9 %shard_map.114 = (f32[8,128,128]{2,1,0:T(8,128)}, f32[8,128,128]{2,1,0:T(8,128)}, f32[8,128,128]{2,1,0:T(8,128)}, bf16[48,128,128]{2,1,0:T(8,128)(2,1)}, f32[8,128,128]{2,1,0:T(8,128)}) custom-call(s32[1]{0:T(128)} %bitcast.2.flag_ref.refs_0_, s32[40]{0:T(128)} %get-tuple-element.28.slot_ref.refs_1_, s32[40]{0:T(128)} %get-tuple-element.29.local_ref.refs_2_, ...), custom_call_target="tpu_custom_call" | custom-call | flops 10000000000 | bytes 10000000 | tf_op jit(solution)/shard_map/pallas_call | solution.py:541
  141.8 25.5 %all_to_all.37 = bf16[16,3,128,128]{3,2,1,0:T(8,128)(2,1)} all-to-all(bf16[16,3,128,128]{3,2,1,0:T(8,128)(2,1)} %bitcast.23), channel_id=1, replica_groups=mesh['seg'=8,'sec'=16] {'sec'}, dimensions={0} | all-to-all | bytes 3145728 | tf_op jit(solution)/shard_map/all_to_all | solution.py:674
  167.3 4.8 %collect.4 = (f32[8,128,128]{2,1,0:T(8,128)}, f32[16,8,128]{2,1,0:T(8,128)}) custom-call(s32[40]{0:T(128)} %get-tuple-element.27.refs_0_, s32[8]{0:T(128)} %dynamic_slice.6.left_ref.refs_1_, s32[32]{0:T(128)} %reshape.37.right_ref.refs_2_, bf16[48,128,128]{2,1,0:T(8,128)(2,1)} %bitcast.18, f32[8,128,128]{2,1,0:T(8,128)} %get-tuple-element.38.refs_4_, ...), custom_call_target="tpu_custom_call" | custom-call | flops 10000000 | bytes 4000000 | tf_op jit(solution)/shard_map/collect/pallas_call | solution.py:616
  172.1 11.8 %all_to_all.38.refs_8_ = f32[16,8,128]{2,1,0:T(8,128)} all-to-all(f32[16,8,128]{2,1,0:T(8,128)} %get-tuple-element.42), channel_id=1, replica_groups=mesh['seg'=8,'sec'=16] {'sec'}, dimensions={0} | all-to-all | bytes 131072 | tf_op jit(solution)/shard_map/all_to_all | solution.py:674
  183.9 12.3 %shard_map.115 = (f32[8,128,128]{2,1,0:T(8,128)}, f32[8,128,128]{2,1,0:T(8,128)}, f32[8,128,128]{2,1,0:T(8,128)}, bf16[48,128,128]{2,1,0:T(8,128)(2,1)}, f32[8,128,128]{2,1,0:T(8,128)}) custom-call(s32[1]{0:T(128)} %bitcast.2.flag_ref.refs_0_, s32[40]{0:T(128)} %get-tuple-element.28.slot_ref.refs_1_, s32[40]{0:T(128)} %get-tuple-element.29.local_ref.refs_2_, ...), custom_call_target="tpu_custom_call" | custom-call | flops 10000000000 | bytes 10000000 | tf_op jit(solution)/shard_map/pallas_call | solution.py:541
  196.2 23.5 %all_to_all.39 = bf16[16,3,128,128]{3,2,1,0:T(8,128)(2,1)} all-to-all(bf16[16,3,128,128]{3,2,1,0:T(8,128)(2,1)} %bitcast.22), channel_id=1, replica_groups=mesh['seg'=8,'sec'=16] {'sec'}, dimensions={0} | all-to-all | bytes 3145728 | tf_op jit(solution)/shard_map/all_to_all | solution.py:674
  219.7 3.9 %collect.5 = (f32[8,128,128]{2,1,0:T(8,128)}, f32[16,8,128]{2,1,0:T(8,128)}) custom-call(s32[40]{0:T(128)} %get-tuple-element.27.refs_0_, s32[8]{0:T(128)} %dynamic_slice.6.left_ref.refs_1_, s32[32]{0:T(128)} %reshape.37.right_ref.refs_2_, bf16[48,128,128]{2,1,0:T(8,128)(2,1)} %bitcast.16, f32[8,128,128]{2,1,0:T(8,128)} %get-tuple-element.45.refs_4_, ...), custom_call_target="tpu_custom_call" | custom-call | flops 10000000 | bytes 4000000 | tf_op jit(solution)/shard_map/collect/pallas_call | solution.py:616
  223.6 11.8 %all_to_all.40.gram_ref = f32[16,8,128]{2,1,0:T(8,128)} all-to-all(f32[16,8,128]{2,1,0:T(8,128)} %get-tuple-element.49), channel_id=1, replica_groups=mesh['seg'=8,'sec'=16] {'sec'}, dimensions={0} | all-to-all | bytes 131072 | tf_op jit(solution)/shard_map/all_to_all | solution.py:674
  235.4 2.6 %finish.1 = (f32[8,64,256]{2,1,0:T(8,128)}, f32[1]{0:T(128)}) custom-call(f32[16,8,128]{2,1,0:T(8,128)} %all_to_all.40.gram_ref, f32[8,128,128]{2,1,0:T(8,128)} %get-tuple-element.48.refs_7_.x_ref, f32[8,128,128]{2,1,0:T(8,128)} %get-tuple-element.47.refs_6_.d_ref), custom_call_target="tpu_custom_call" | custom-call | flops 1000000 | bytes 2000000 | tf_op jit(solution)/shard_map/finish/pallas_call | solution.py:655
  (27 shorter events, 9.2 us)
Async XLA Ops:
  0.6 57.5 %copy-start = (s32[128,4]{0,1:T(4,128)S(1)}, s32[128,4]{0,1:T(4,128)}, u32[]{:S(2)}) copy-start(s32[128,4]{0,1:T(4,128)} %param.19) | copy-start | bytes 6148
  5.5 8.3 %copy-start.1 = (bf16[1,8,64,1920]{3,2,1,0:T(8,128)(2,1)S(1)}, bf16[1,8,64,1920]{3,2,1,0:T(8,128)(2,1)}, u32[]{:S(2)}) copy-start(bf16[1,8,64,1920]{3,2,1,0:T(8,128)(2,1)} %param.11) | copy-start | bytes 5898244
  5.5 10.2 %copy-start.3 = (s32[30,30]{1,0:T(8,128)S(1)}, s32[30,30]{1,0:T(8,128)}, u32[]{:S(2)}) copy-start(s32[30,30]{1,0:T(8,128)} %param.16) | copy-start | bytes 10804
  5.6 10.2 %copy-start.2 = (bf16[30,4,30,4]{2,3,1,0:T(4,128)(2,1)S(1)}, bf16[30,4,30,4]{2,3,1,0:T(4,128)(2,1)}, u32[]{:S(2)}) copy-start(bf16[30,4,30,4]{2,3,1,0:T(4,128)(2,1)} %param.15) | copy-start | bytes 86404
  5.6 32.8 %all-to-all-start = ((bf16[16,3,64,256]{3,2,1,0:T(8,128)(2,1)}), bf16[16,3,64,256]{3,2,1,0:T(8,128)(2,1)}, u32[]{:S(2)}, u32[]{:S(2)}) async-start(bf16[16,3,64,256]{3,2,1,0:T(8,128)(2,1)} %get-tuple-element.30), calls=%async_computation | async-start | bytes 3145728 | tf_op jit(solution)/shard_map/all_to_all | solution.py:674
  13.8 49.2 %collective-permute-start = (bf16[8,64,1920]{2,1,0:T(8,128)(2,1)S(1)}, bf16[8,64,1920]{2,1,0:T(8,128)(2,1)}, u32[]{:S(2)}, u32[]{:S(2)}) collective-permute-start(bf16[8,64,1920]{2,1,0:T(8,128)(2,1)S(1)} %bitcast.21), channel_id=1, source_target_pairs={{16,0},{32,16},{48,32},{64,48},{80,64},{96,80},{112,96},{17,1},{33... | collective-permute-start | bytes 5898248 | tf_op jit(solution)/shard_map/ppermute | solution.py:32
  45.4 12.9 %copy-start.5 = (s32[128]{0:T(128)S(1)}, s32[128]{0:T(128)}, u32[]{:S(2)}) copy-start(s32[128]{0:T(128)} %param.18) | copy-start | bytes 1540
  45.4 31.7 %collective-permute-start.1 = (bf16[4,960,128]{2,1,0:T(8,128)(2,1)}, bf16[4,960,128]{2,1,0:T(8,128)(2,1)S(1)}, u32[]{:S(2)}, u32[]{:S(2)}) collective-permute-start(bf16[4,960,128]{2,1,0:T(8,128)(2,1)} %build_environment.2), channel_id=1, source_target_pairs={{0,16},{16,32},{32,48},{48,64},{64,80},{80,96},{96,112},{1,17},{17... | collective-permute-start | bytes 2949128 | tf_op jit(solution)/shard_map/ppermute | solution.py:32
  54.5 22.6 %collective-permute-start.2 = (bf16[4,960,128]{2,1,0:T(8,128)(2,1)}, bf16[4,960,128]{2,1,0:T(8,128)(2,1)}, u32[]{:S(2)}, u32[]{:S(2)}) collective-permute-start(bf16[4,960,128]{2,1,0:T(8,128)(2,1)} %build_environment.3), channel_id=1, source_target_pairs={{0,16},{16,32},{32,48},{48,64},{64,80},{80,96},{96,112},{1,17},{17... | collective-permute-start | bytes 2949128 | tf_op jit(solution)/shard_map/ppermute | solution.py:32
  77.1 1.0 copy-start.4
